TPU v7x, 512 devices: a whole 4x4x16 slice. The times are simulated.
512 devices in a mesh: section: 8 (over x, z_hi), seq: 64 (over y, z_lo, core).
Axes of the slice: x: 4, y: 4, z: 16 (z_hi: 2, z_lo: 8; z = z_hi * 8 + z_lo), core: 2. Of those that a mesh axis runs over, the one named last changes fastest.
Arguments:
- queries: bfloat16 [8, 256, 2048], P('section', 'seq'), may hold values from -120 to 120
- keys_values: bfloat16 [8, 16384, 4096], P('section', 'seq'), may hold values from -41 to 41
- enc_len: int32 [8], P('section'), may hold values from 4096 to 16384, as said below
- order: int32 [8], replicated, may hold values from 0 to 7, each once
- d_out: bfloat16 [8, 256, 2048], P('section', 'seq'), may hold values from -6 to 6
Outputs:
- attended: bfloat16 [8, 256, 2048], P('section', 'seq')
- d_queries: bfloat16 [8, 256, 2048], P('section', 'seq')
- d_keys_values: bfloat16 [8, 16384, 4096], P('section', 'seq')
Inputs may be any that keep to these rules, and one draw needn't show every extreme that they name: Positions from enc_len on are padding; some micro-batch has exactly 16384 valid positions. `order`: every micro-batch is run by exactly one group.
All inputs are finite; a program needn't handle non-finite values.
Results may differ from a plain program's by a relative error of at most 0.0049.
Values may be sent and summed in bfloat16 or wider, within the bound.
A program may use at most 64 MiB of HBM per device.

v0:
```python
import math

import jax
import jax.numpy as jnp
from jax import lax
from jax.sharding import PartitionSpec as P

HD = 256


def combined_all(shard, axis, combine):
    everything = jax.tree.map(lambda part: lax.all_gather(part, axis), shard)
    initial = jax.tree.map(lambda part: part[0], everything)

    def step(k, so_far):
        return combine(so_far, jax.tree.map(lambda part: part[k], everything))

    return lax.fori_loop(1, lax.axis_size(axis), step, initial)


def combine_stats(first, second):
    top = jnp.maximum(first[0], second[0])
    total = first[1] * jnp.exp(first[0] - top) + second[1] * jnp.exp(second[0] - top)
    return (top, total)


def shards(queries, keys_values, enc_len, order, d_out):
    score_scale = 1.0 / math.sqrt(HD)
    section_count = lax.axis_size("section")
    my_section = lax.axis_index("section")
    seq_index = lax.axis_index("seq")
    slots = jnp.arange(section_count, dtype=jnp.int32)
    my_batch = jnp.sum(jnp.where(slots == my_section, order, 0))
    source = jnp.sum(jnp.where(order == my_section, slots, 0))
    to_batch = (slots == my_batch)[:, None, None]
    zero_bf = jnp.zeros((), jnp.bfloat16)
    query_send = jnp.where(to_batch, queries[0][None], zero_bf)
    grad_send = jnp.where(to_batch, d_out[0][None], zero_bf)
    query_recv, grad_recv = (
        lax.all_to_all(query_send, "section", split_axis=0, concat_axis=0, tiled=True),
        lax.all_to_all(grad_send, "section", split_axis=0, concat_axis=0, tiled=True),
    )
    query_local = jnp.sum(query_recv, axis=0, dtype=jnp.bfloat16)
    grad_local = jnp.sum(grad_recv, axis=0, dtype=jnp.bfloat16)
    query_all, grad_all = (
        lax.all_gather(query_local, "seq", axis=0, tiled=True),
        lax.all_gather(grad_local, "seq", axis=0, tiled=True),
    )
    local_rows = keys_values.shape[1]
    tq_rows = queries.shape[1]
    attn_width = keys_values.shape[2] // 2
    head_count = attn_width // HD
    memory = keys_values[0]
    key_heads = memory[:, :attn_width].reshape(local_rows, head_count, HD)
    value_heads = memory[:, attn_width:].reshape(local_rows, head_count, HD)
    query_heads = query_all.reshape(-1, head_count, HD)
    grad_heads = grad_all.reshape(-1, head_count, HD)
    length = enc_len[0]
    first_key = seq_index * local_rows
    key_valid = jnp.arange(local_rows, dtype=jnp.int32) + first_key < length
    scores = (
        jnp.einsum("ihd,jhd->hij", query_heads, key_heads, preferred_element_type=jnp.float32)
        * score_scale
    )
    scores = jnp.where(key_valid[None, None, :], scores, -jnp.inf)
    local_max = jnp.maximum(jnp.max(scores, axis=-1), -1e30)
    local_sum = jnp.sum(jnp.exp(scores - local_max[..., None]), axis=-1)
    whole_max, whole_sum = combined_all((local_max, local_sum), "seq", combine_stats)
    probabilities = jnp.exp(scores - whole_max[..., None]) / whole_sum[..., None]
    weights = probabilities.astype(jnp.bfloat16)
    result = jnp.einsum("hij,jhd->ihd", weights, value_heads, preferred_element_type=jnp.float32)
    attended_sum = lax.psum_scatter(
        result.reshape(tq_rows * lax.axis_size("seq"), attn_width),
        "seq",
        scatter_dimension=0,
        tiled=True,
    )
    dprobs = jnp.einsum("ihd,jhd->hij", grad_heads, value_heads, preferred_element_type=jnp.float32)
    delta = lax.psum(jnp.sum(probabilities * dprobs, axis=-1), "seq")
    dscores = (probabilities * (dprobs - delta[..., None]) * score_scale).astype(jnp.bfloat16)
    result = jnp.einsum("hij,jhd->ihd", dscores, key_heads, preferred_element_type=jnp.float32)
    query_sum = lax.psum_scatter(
        result.reshape(tq_rows * lax.axis_size("seq"), attn_width),
        "seq",
        scatter_dimension=0,
        tiled=True,
    )
    attended = attended_sum.astype(jnp.bfloat16)
    d_queries = query_sum.astype(jnp.bfloat16)
    key_grad = jnp.einsum("hij,ihd->jhd", dscores, query_heads, preferred_element_type=jnp.float32)
    value_grad = jnp.einsum("hij,ihd->jhd", weights, grad_heads, preferred_element_type=jnp.float32)
    joined = jnp.concatenate(
        [key_grad.reshape(local_rows, attn_width), value_grad.reshape(local_rows, attn_width)],
        axis=1,
    )
    d_memory = joined.astype(jnp.bfloat16)
    to_source = (slots == source)[:, None, None]
    attended_back = jnp.where(to_source, attended[None], zero_bf)
    queries_back = jnp.where(to_source, d_queries[None], zero_bf)
    attended_home, queries_home = (
        lax.all_to_all(attended_back, "section", split_axis=0, concat_axis=0, tiled=True),
        lax.all_to_all(queries_back, "section", split_axis=0, concat_axis=0, tiled=True),
    )
    attended_out = jnp.sum(attended_home, axis=0, dtype=jnp.bfloat16)
    queries_out = jnp.sum(queries_home, axis=0, dtype=jnp.bfloat16)
    return (attended_out[None], queries_out[None], d_memory[None])


def solution(mesh):
    placed = (
        P("section", "seq", None),
        P("section", "seq", None),
        P("section"),
        P(),
        P("section", "seq", None),
    )
    return jax.shard_map(
        shards,
        mesh=mesh,
        in_specs=placed,
        out_specs=(P("section", "seq", None), P("section", "seq", None), P("section", "seq", None)),
        check_vma=False,
    )
```

profile of v0, /device:TPU:1, one launch (start us, length us, event | category | flops | bytes accessed | tf_op | source)
XLA Modules:
  0.0 1194.0 jit_solution(6223347452346712044)
XLA Ops:
  11.4 32.1 %all_to_all.20 = bf16[8,4,2048]{2,1,0:T(4,128)(2,1)S(1)} all-to-all(bf16[8,4,2048]{2,1,0:T(4,128)(2,1)S(1)} %get-tuple-element.159), channel_id=1, replica_groups=mesh['section'=8,'seq'=64] {'section'}, dimensions={0} | all-to-all | bytes 262144 | tf_op jit(solution)/shard_map/all_to_all | solution.py:40
  44.2 3.4 all-to-all-start.2
  47.6 3.3 copy.86
  55.1 6.8 all-to-all-done.2
  62.6 97.5 %all-gather.7.cloned.1.call-done = bf16[64,4,2048]{2,1,0:T(4,128)(2,1)} async-done(((bf16[1,4,2048]{2,1,0:T(4,128)(2,1)}), bf16[64,4,2048]{2,1,0:T(4,128)(2,1)}) %all-gather.7.cloned.1.call-update) | async-done | bytes 1048592 | tf_op jit(solution)/shard_map/all_gather | solution.py:46
  162.6 1.8 fusion.8
  164.5 119.1 %all-gather = f32[512,256]{1,0:T(8,128)S(1)} all-gather(f32[8,256]{1,0:T(8,128)S(1)} %broadcast_maximum_fusion), channel_id=2, replica_groups=mesh['section'=8,'seq'=64] {'seq'}, dimensions={0}, use_global_device_ids=true | all-gather | bytes 532480 | tf_op jit(solution)/shard_map/all_gather | solution.py:12
  283.8 114.5 %all-gather.1 = f32[512,256]{1,0:T(8,128)S(1)} all-gather(f32[8,256]{1,0:T(8,128)S(1)} %exponential_reduce_fusion), channel_id=3, replica_groups=mesh['section'=8,'seq'=64] {'seq'}, dimensions={0}, use_global_device_ids=true | all-gather | bytes 532480 | tf_op jit(solution)/shard_map/all_gather | solution.py:12
  399.1 47.4 %while.17 = (s32[]{:T(128)}, f32[8,256]{1,0:T(8,128)S(1)}, f32[8,256]{1,0:T(8,128)S(1)}, f32[64,8,256]{2,1,0:T(8,128)}, f32[64,8,256]{2,1,0:T(8,128)}, /*index=5*/s32[]{:T(128)}, s32[]{:T(128)}, s32[]{:T(128)}) while((s32[]{:T(128)}, f32[8,256]{1,0:T(8,128)S(1)}, f32[8,256]{1,0:T(8,128)S(1)}, f32[64,8,256]{2,1,0:T(8,128)}, ...), condition=%wide.region_6.7_spmd, body=%wide.region_5.6_spmd.sunk | while | flops 12293 | bytes 49283 | solution.py:18
  446.6 2.6 reshape.93
  449.2 2.4 copy.100
  451.6 3.2 fusion.3
  454.8 2.0 multiply_reduce_fusion
  456.8 212.0 %psum.7 = f32[8,256]{1,0:T(8,128)S(1)} all-reduce(f32[8,256]{1,0:T(8,128)S(1)} %get-tuple-element.162), channel_id=1, replica_groups=mesh['section'=8,'seq'=64] {'seq'}, use_global_device_ids=true, to_apply=%region_11.12 | all-reduce | flops 2048 | bytes 16384 | tf_op jit(solution)/shard_map/psum | solution.py:79
  668.8 2.2 multiply_convert_fusion
  672.9 461.7 %all-reduce.4 = (bf16[256,2048]{0,1:T(8,128)(2,1)}, bf16[256,2048]{0,1:T(8,128)(2,1)}) all-reduce(f32[256,2048]{0,1:T(8,128)} %bitcast.59, f32[256,2048]{0,1:T(8,128)} %bitcast.57), channel_id=4, replica_groups=mesh['section'=8,'seq'=64] {'seq'}, use_global_device_ids=true, to_apply=%region_7.8.clone | all-reduce | flops 1048576 | bytes 6291456
  1134.5 2.0 constant_dynamic-slice_fusion.1
  1137.8 2.1 constant_dynamic-slice_fusion
  1142.0 10.1 all-to-all-start.1
  1152.1 2.8 convolution_convert_fusion
  1154.9 2.4 copy.103
  1158.4 8.0 all-to-all-done.1
  1166.3 5.9 all-to-all-start.3
  1174.4 12.1 %all-to-all-done.3 = bf16[8,4,2048]{2,1,0:T(4,128)(2,1)S(1)} async-done(((bf16[8,4,2048]{2,1,0:T(4,128)(2,1)}), bf16[8,4,2048]{2,1,0:T(4,128)(2,1)S(1)}, u32[]{:S(2)}, u32[]{:S(2)}) %all-to-all-start.3) | async-done | bytes 131104 | tf_op jit(solution)/shard_map/all_to_all | solution.py:102
  (107 shorter events, 67.3 us)
Async XLA Ops:
  7.2 152.9 %all-gather.7.cloned.1.call-start = ((), (), s32[]{:S(2)}) async-start(), calls=%async_computation.4 | async-start | bytes 1064960 | tf_op jit(solution)/shard_map/all_gather | solution.py:46
  44.2 17.7 %all-to-all-start.2 = ((bf16[8,4,2048]{2,1,0:T(4,128)(2,1)}), bf16[8,4,2048]{2,1,0:T(4,128)(2,1)S(1)}, u32[]{:S(2)}, u32[]{:S(2)}) async-start(bf16[8,4,2048]{2,1,0:T(4,128)(2,1)} %get-tuple-element.158), calls=%async_computation.2 | async-start | bytes 262144 | tf_op jit(solution)/shard_map/all_to_all | solution.py:41
  47.6 399.0 %all-gather.9.cloned.1.call-start = ((), (), s32[]{:S(2)}) async-start(), calls=%async_computation.5 | async-start | bytes 1064960 | tf_op jit(solution)/shard_map/all_gather | solution.py:47
  283.5 114.8 %copy-start.6 = (f32[512,256]{1,0:T(8,128)}, f32[512,256]{1,0:T(8,128)S(1)}, u32[]{:S(2)}) copy-start(f32[512,256]{1,0:T(8,128)S(1)} %all-gather) | copy-start | bytes 1572868
  398.3 0.8 copy-start.7
  451.6 3.2 copy-start.4
  451.6 3.2 copy-start.5
  668.8 2.2 copy-start.2
  671.0 1.8 copy-start
  1142.0 24.3 %all-to-all-start.1 = ((bf16[8,4,2048]{2,1,0:T(4,128)(2,1)}), bf16[8,4,2048]{2,1,0:T(4,128)(2,1)S(1)}, u32[]{:S(2)}, u32[]{:S(2)}) async-start(bf16[8,4,2048]{2,1,0:T(4,128)(2,1)} %get-tuple-element.157), calls=%async_computation.1 | async-start | bytes 262144 | tf_op jit(solution)/shard_map/all_to_all | solution.py:101
  1154.9 2.4 copy-start.1
  1157.7 14.5 %copy-start.3 = (bf16[1,256,2048]{2,1,0:T(8,128)(2,1)S(1)}, bf16[1,256,2048]{2,1,0:T(8,128)(2,1)}, u32[]{:S(2)}) copy-start(bf16[1,256,2048]{2,1,0:T(8,128)(2,1)} %copy.103) | copy-start | bytes 3145732
  1166.3 20.2 %all-to-all-start.3 = ((bf16[8,4,2048]{2,1,0:T(4,128)(2,1)}), bf16[8,4,2048]{2,1,0:T(4,128)(2,1)S(1)}, u32[]{:S(2)}, u32[]{:S(2)}) async-start(bf16[8,4,2048]{2,1,0:T(4,128)(2,1)} %get-tuple-element.156), calls=%async_computation.3 | async-start | bytes 262144 | tf_op jit(solution)/shard_map/all_to_all | solution.py:102
Sparse Core Ops, SparseCore 0:
  44.3 115.6 all-gather.6
  162.8 115.5 all-gather.8
where the time goes:
time: 1210 us; the launch traced here: 1190 us
  blocking collectives  939 us (78%)
  waiting for transfers between devices  124 us (10%)
  other arithmetic  57.8 us (5%)
  local copies, waits for them, and re-layouts  24.1 us (2%)
  starting transfers between devices  19.4 us (2%)
  between operations  15.6 us (1%)
  matrix products  12.1 us (1%)
    unnamed x1, blocking collectives  462 us
    all_gather x2, blocking collectives, combined_all(): everything = jax.tree.map(lambda part: lax.all_gather(part, axis), shard)  234 us
    psum x1, blocking collectives, shards(): delta = lax.psum(jnp.sum(probabilities * dprobs, axis=-1), 'seq')  212 us
    all_gather x1, waiting for transfers between devices, shards(): lax.all_gather(query_local, 'seq', axis=0, tiled=True)  97.5 us
    add x63, other arithmetic, combine_stats(): first[1] * jnp.exp(first[0] - top) + second[1] * jnp.exp(second[0] - top)  46.1 us
    all_to_all x1, blocking collectives, shards(): lax.all_to_all(query_send, 'section', split_axis=0, concat_axis=0, tiled=...  32.1 us
  transfers between devices with their start and end apart: 5, of which 4 were waited for; matrix products, arithmetic and copies ran while one was open for 6% of the time, Pallas kernels for 0%

commit v1 on v0

v1 whole, which is shorter than its diff:
```python
import functools
import math

import jax
import jax.numpy as jnp
from jax import lax
from jax.experimental import pallas as pl
from jax.experimental.pallas import tpu as pltpu
from jax.sharding import PartitionSpec as P

MESH = pl.DeviceIdType.MESH
HD = 256
NX, NY, NZ = 4, 4, 8
BF = jnp.bfloat16
F32 = jnp.float32


def mod(a, n):
    return lax.rem(a, jnp.int32(n))


def merge(parts):
    top = functools.reduce(jnp.maximum, [p[0] for p in parts])
    scale = [jnp.exp(p[0] - top) for p in parts]
    total = sum(p[1] * s for p, s in zip(parts, scale))
    dots = sum(p[2] * s for p, s in zip(parts, scale))
    return top, total, dots


def kernel(
    q_ref, kv_ref, len_ref, ord_ref, g_ref,
    att_ref, dq_ref, dkv_ref,
    qv, xb0, xb1, rows8, sb, own, pb, gb, dense, kvv, ev, dv,
    st, sy, szc, szq, st2, st3,
    wv, dsv, of, sd, sd2, rr, ry, ys, zs, zq, zt, zc, rt, rb0, rb1, psd, prb, dkvs,
    load_sem, xs_sem, xr_sem, kvs_sem, kvr_sem, ps_sem, pr_sem, zs_sem, zr_sem,
    ys_sem, yr_sem, ss_sem, sr_sem, as_sem, ar_sem, bs_sem, br_sem, ts_sem, tr_sem, ds_sem, dr_sem,
):
    sec = lax.axis_index("section")
    seq = lax.axis_index("seq")
    x, h = lax.div(sec, jnp.int32(2)), mod(sec, 2)
    y, zl, c = lax.div(seq, jnp.int32(16)), mod(lax.div(seq, jnp.int32(2)), NZ), mod(seq, 2)
    xb, rb = (xb0, xb1), (rb0, rb1)
    half = att_ref.shape[2] // 2
    heads = half // HD
    keys = kv_ref.shape[1]
    width = half * 2
    score_scale = 1.0 / math.sqrt(HD)
    quad, zin = lax.div(zl, jnp.int32(4)) * 4, mod(zl, 4)
    zx = mod(zl + 4, NZ)

    def dev(xx, hh, yy, zz, cc):
        return (xx * 2 + hh, (yy * NZ + zz) * 2 + cc)

    def zto(d):
        return quad + mod(zin + d, 4)

    def zfrom(d):
        return quad + mod(zin + 4 - d, 4)

    def slot(r):
        base = zfrom(r % 4)
        return base if r < 4 else mod(base + 4, NZ)

    def ynb(d):
        return mod(y + d + NY, NY)

    other = 1 - c
    core_of = lambda dc: c if dc == 0 else other
    x_peers = [(dx, dc) for dx in range(NX) for dc in range(2) if dx or dc]
    partner = dev(x, 1 - h, y, zx, c)
    pending = []

    def send(src, dst, ssem, rsem, target):
        copy = pltpu.make_async_remote_copy(
            src_ref=src, dst_ref=dst, send_sem=ssem, recv_sem=rsem, device_id=target, device_id_type=MESH
        )
        copy.start()
        pending.append(copy)

    def arrive(dst, ssem, rsem):
        pltpu.make_async_remote_copy(
            src_ref=dst, dst_ref=dst, send_sem=ssem, recv_sem=rsem, device_id=partner, device_id_type=MESH
        ).wait_recv()

    barrier = pltpu.get_barrier_semaphore()
    peers = [dev(mod(x + dx, NX), h, y, zl, core_of(dc)) for dx, dc in x_peers]
    peers += [dev(x, h, ynb(d), zl, c) for d in (1, 2, -1)]
    peers += [dev(x, h, y, zto(d), c) for d in (1, 2, 3)]
    peers += [dev(x, h, y, zx, c), partner]
    for peer in peers:
        pl.semaphore_signal(barrier, inc=1, device_id=peer, device_id_type=MESH)
    load_q = [
        pltpu.make_async_copy(ref.at[0], qv.at[a], load_sem.at[a]) for a, ref in enumerate((q_ref, g_ref))
    ]
    for copy in load_q:
        copy.start()
    my_cols = [pl.multiple_of(b * width + c * half, HD) for b in range(2)]
    their_cols = [pl.multiple_of(b * width + other * half, HD) for b in range(2)]
    my_keys = pl.ds(pl.multiple_of(c * keys, keys), keys)
    load_kv = []
    for b in range(2):
        for n in range(heads):
            copy = pltpu.make_async_copy(
                kv_ref.at[0, :, pl.ds(my_cols[b] + n * HD, HD)], kvv.at[b, n, my_keys], load_sem.at[2 + b * heads + n]
            )
            copy.start()
            load_kv.append(copy)
    for copy in load_q:
        copy.wait()
    pl.semaphore_wait(barrier, len(peers))

    for a in range(2):
        for dx, dc in x_peers:
            k = dx * 2 + dc
            cc = core_of(dc)
            send(
                qv.at[a, :, pl.ds(pl.multiple_of(cc * half, half), half)],
                xb[a].at[k], xs_sem.at[k, a], xr_sem.at[k, a],
                dev(mod(x + dx, NX), h, y, zl, cc),
            )
    own_copy = [
        pltpu.make_async_copy(
            qv.at[a, :, pl.ds(pl.multiple_of(c * half, half), half)], xb[a].at[0], load_sem.at[2 + 4 * heads + a]
        )
        for a in range(2)
    ]
    for copy in own_copy:
        copy.start()
    for b in range(2):
        for n in range(heads):
            send(
                kv_ref.at[0, :, pl.ds(their_cols[b] + n * HD, HD)], kvv.at[b, n, my_keys],
                kvs_sem.at[b, n], kvr_sem.at[b, n], dev(x, h, y, zl, other),
            )

    def inverse(section):
        found = jnp.int32(0)
        for k in range(2 * NX):
            found = jnp.where(ord_ref[k] == section, jnp.int32(k), found)
        return found

    twin = x * 2 + (1 - h)
    src_mine, src_twin = inverse(sec), inverse(twin)

    def pick(section, a):
        k = mod(x - lax.div(section, jnp.int32(2)) + NX, NX) * 2
        rows8[0:4, :] = xb[a][k + c].astype(F32)
        rows8[4:8, :] = xb[a][k + other].astype(F32)
        return rows8[...].astype(BF)

    for a in range(2):
        own_copy[a].wait()
        for dx, dc in x_peers:
            k = dx * 2 + dc
            arrive(xb[a].at[k], xs_sem.at[k, a], xr_sem.at[k, a])
        sb[a] = pick(src_twin, a)
        send(sb.at[a], pb.at[a], ps_sem.at[a], pr_sem.at[a], partner)
    for a in range(2):
        own[a] = pick(src_mine, a)
    mine_here = mod(src_mine, 2) == h

    def to_quad(r, a):
        b = r // 4
        for d in (1, 2, 3):
            send(
                gb.at[y, slot(r), a], gb.at[y, slot(r), a], zs_sem.at[d + 4 * b, a], zr_sem.at[d + 4 * b, a],
                dev(x, h, y, zto(d), c),
            )

    def to_y(r, a):
        for i, d in enumerate((1, -1)):
            send(
                gb.at[y, slot(r), a], gb.at[y, slot(r), a], ys_sem.at[i, r, a], yr_sem.at[i, r, a],
                dev(x, h, ynb(d), zl, c),
            )

    def relay_y(r, a):
        d = 1 if a == 0 else -1
        arrive(gb.at[ynb(-d), slot(r), a], ys_sem.at[a, r, a], yr_sem.at[a, r, a])
        send(
            gb.at[ynb(-d), slot(r), a], gb.at[ynb(-d), slot(r), a], ys_sem.at[2, r, a], yr_sem.at[2, r, a],
            dev(x, h, ynb(d), zl, c),
        )

    def z_arrive(r, a):
        arrive(gb.at[y, slot(r), a], zs_sem.at[r, a], zr_sem.at[r, a])

    for a in range(2):
        arrive(pb.at[a], ps_sem.at[a], pr_sem.at[a])
        gb[y, zl, a] = jnp.where(mine_here, own[a], pb[a])
        send(gb.at[y, zl, a], gb.at[y, zl, a], zs_sem.at[4, a], zr_sem.at[4, a], dev(x, h, y, zx, c))
        to_quad(0, a)
        to_y(0, a)
    for a in range(2):
        z_arrive(4, a)
        to_quad(4, a)
        to_y(4, a)
    for r in (1, 2, 3):
        for a in range(2):
            z_arrive(r, a)
            to_y(r, a)
    for r in (0, 4):
        for a in range(2):
            relay_y(r, a)
    for r in (5, 6, 7):
        for a in range(2):
            z_arrive(r, a)
            to_y(r, a)
    for r in (1, 2, 3, 5, 6, 7):
        for a in range(2):
            relay_y(r, a)
    for copy in load_kv:
        copy.wait()
    for b in range(2):
        for n in range(heads):
            arrive(kvv.at[b, n, pl.ds(pl.multiple_of(other * keys, keys), keys)], kvs_sem.at[b, n], kvr_sem.at[b, n])
    for r in range(NZ):
        for a in range(2):
            i = 1 - a
            arrive(gb.at[ynb(1 if i else -1), slot(r), a], ys_sem.at[i, r, a], yr_sem.at[i, r, a])
            arrive(gb.at[ynb(2), slot(r), a], ys_sem.at[2, r, a], yr_sem.at[2, r, a])

    first_key = (y * NZ + zl) * (2 * keys)
    key_at = lax.broadcasted_iota(jnp.int32, (2 * keys, HD), 0) + first_key
    valid = key_at < len_ref[0]
    nt = (((1,), (1,)), ((), ()))
    nn = (((1,), (0,)), ((), ()))
    tn = (((0,), (0,)), ((), ()))
    targets = NY * NZ * 8
    for n in range(heads):
        for a in range(2):
            block = gb[:, :, a, :, n * HD : (n + 1) * HD].astype(F32)
            dense[a, n] = block.reshape(targets, HD).astype(BF)
        scores = lax.dot_general(kvv[0, n], dense[0, n], nt, preferred_element_type=F32) * score_scale
        scores = jnp.where(valid, scores, -jnp.inf)
        top = jnp.maximum(jnp.max(scores, axis=0, keepdims=True), -1e30)
        e = jnp.exp(scores - top)
        dp = lax.dot_general(kvv[1, n], dense[1, n], nt, preferred_element_type=F32)
        ev[n] = e
        dv[n] = dp
        st[0, n : n + 1, :] = top
        st[1, n : n + 1, :] = jnp.sum(e, axis=0, keepdims=True)
        st[2, n : n + 1, :] = jnp.sum(e * dp, axis=0, keepdims=True)

    for i, d in enumerate((1, 2, -1)):
        send(st, sy.at[i], ss_sem.at[i], sr_sem.at[i], dev(x, h, ynb(d), zl, c))
    for i in range(3):
        arrive(sy.at[i], ss_sem.at[i], sr_sem.at[i])
    part = merge([(st[0], st[1], st[2])] + [(sy[i, 0], sy[i, 1], sy[i, 2]) for i in range(3)])
    for i in range(3):
        st2[i] = part[i]
    send(st2, szc, ss_sem.at[3], sr_sem.at[3], dev(x, h, y, zx, c))
    arrive(szc, ss_sem.at[3], sr_sem.at[3])
    part = merge([part, (szc[0], szc[1], szc[2])])
    for i in range(3):
        st3[i] = part[i]
    for d in (1, 2, 3):
        send(st3, szq.at[d - 1], ss_sem.at[3 + d], sr_sem.at[3 + d], dev(x, h, y, zto(d), c))
    for d in (1, 2, 3):
        arrive(szq.at[d - 1], ss_sem.at[3 + d], sr_sem.at[3 + d])
    whole_max, whole_sum, dots = merge([part] + [(szq[i, 0], szq[i, 1], szq[i, 2]) for i in range(3)])
    inv_sum = 1.0 / whole_sum
    delta = dots * inv_sum
    factor = jnp.exp(st[0] - whole_max) * inv_sum

    for n in range(heads):
        p = ev[n] * factor[n : n + 1, :]
        wv[n] = p.astype(BF)
        dsv[n] = (p * (dv[n] - delta[n : n + 1, :]) * score_scale).astype(BF)
        for a in range(2):
            d = 1 if a == 0 else -1
            out = lax.dot_general(
                (wv if a == 0 else dsv)[n], kvv[1 - a, n], tn, preferred_element_type=F32
            )
            of[a, n] = out.reshape(NY, NZ * 8, HD)
            sd[a, n, 0] = of[a, n, ynb(2)].astype(BF)
            send(sd.at[a, n, 0], rr.at[a, n], as_sem.at[a, n, 0], ar_sem.at[a, n, 0], dev(x, h, ynb(d), zl, c))
            sd[a, n, 1] = of[a, n, ynb(-d)].astype(BF)
            send(sd.at[a, n, 1], ry.at[a, n, 1], as_sem.at[a, n, 1], ar_sem.at[a, n, 1], dev(x, h, ynb(-d), zl, c))
    for n in range(heads):
        for a in range(2):
            d = 1 if a == 0 else -1
            arrive(rr.at[a, n], as_sem.at[a, n, 0], ar_sem.at[a, n, 0])
            sd2[a, n] = (rr[a, n].astype(F32) + of[a, n, ynb(d)]).astype(BF)
            send(sd2.at[a, n], ry.at[a, n, 0], as_sem.at[a, n, 2], ar_sem.at[a, n, 2], dev(x, h, ynb(d), zl, c))

    stores = []
    for n in range(heads):
        for b in range(2):
            grad = lax.dot_general((dsv, wv)[b][n], dense[b, n], nn, preferred_element_type=F32)
            dkvs[b, n] = grad.astype(BF)
            copy = pltpu.make_async_copy(
                dkvs.at[b, n, my_keys], dkv_ref.at[0, :, pl.ds(my_cols[b] + n * HD, HD)], load_sem.at[2 + 2 * heads + b * heads + n]
            )
            copy.start()
            stores.append(copy)
            send(
                dkvs.at[b, n, pl.ds(pl.multiple_of(other * keys, keys), keys)],
                dkv_ref.at[0, :, pl.ds(my_cols[b] + n * HD, HD)],
                ds_sem.at[b, n], dr_sem.at[b, n], dev(x, h, y, zl, other),
            )

    for a in range(2):
        for n in range(heads):
            arrive(ry.at[a, n, 0], as_sem.at[a, n, 2], ar_sem.at[a, n, 2])
            arrive(ry.at[a, n, 1], as_sem.at[a, n, 1], ar_sem.at[a, n, 1])
            total = of[a, n, y] + ry[a, n, 0].astype(F32) + ry[a, n, 1].astype(F32)
            ys[a, :, :, n * HD : (n + 1) * HD] = total.reshape(NZ, 8, HD)
        for d in (1, 2, 3):
            zs[a, d - 1, 0] = ys[a, zto(d)].astype(BF)
            zs[a, d - 1, 1] = ys[a, mod(zto(d) + 4, NZ)].astype(BF)
            send(zs.at[a, d - 1], zq.at[a, d - 1], bs_sem.at[a, d], br_sem.at[a, d], dev(x, h, y, zto(d), c))
    for a in range(2):
        for d in (1, 2, 3):
            arrive(zq.at[a, d - 1], bs_sem.at[a, d], br_sem.at[a, d])
        far = ys[a, zx] + sum(zq[a, i, 1].astype(F32) for i in range(3))
        zt[a] = far.astype(BF)
        send(zt.at[a], zc.at[a], bs_sem.at[a, 0], br_sem.at[a, 0], dev(x, h, y, zx, c))
    for a in range(2):
        near = ys[a, zl] + sum(zq[a, i, 0].astype(F32) for i in range(3))
        arrive(zc.at[a], bs_sem.at[a, 0], br_sem.at[a, 0])
        rows8[...] = near + zc[a].astype(F32)
        rt[0, a] = rows8[0:4, :].astype(BF)
        rt[1, a] = rows8[4:8, :].astype(BF)
        for dx, dc in x_peers:
            k = dx * 2 + dc
            cc = core_of(dc)
            send(
                rt.at[cc, a], rb[a].at[k], ts_sem.at[k, a], tr_sem.at[k, a],
                dev(mod(x + dx, NX), h, y, zl, cc),
            )
        rb[a][0] = rt[c, a]

    ran_mine, ran_twin = ord_ref[sec], ord_ref[twin]

    def fetch(section, a):
        k = mod(x - lax.div(section, jnp.int32(2)) + NX, NX) * 2
        return rb[a][k + c], rb[a][k + other]

    for a in range(2):
        for dx, dc in x_peers:
            k = dx * 2 + dc
            arrive(rb[a].at[k], ts_sem.at[k, a], tr_sem.at[k, a])
        low, high = fetch(ran_twin, a)
        psd[a, :, 0:half] = low
        psd[a, :, half:] = high
        send(psd.at[a], prb.at[a], ts_sem.at[0, a], tr_sem.at[0, a], partner)
    ran_here = mod(ran_mine, 2) == h
    for copy in stores:
        copy.wait()
    for n in range(heads):
        for b in range(2):
            arrive(
                dkv_ref.at[0, :, pl.ds(their_cols[b] + n * HD, HD)], ds_sem.at[b, n], dr_sem.at[b, n]
            )
    for a, out in enumerate((att_ref, dq_ref)):
        low, high = fetch(ran_mine, a)
        arrive(prb.at[a], ts_sem.at[0, a], tr_sem.at[0, a])
        out[0, :, 0:half] = jnp.where(ran_here, low, prb[a, :, 0:half])
        out[0, :, half:] = jnp.where(ran_here, high, prb[a, :, half:])
    for copy in pending:
        copy.wait_send()


def shards(queries, keys_values, enc_len, order, d_out):
    rows, width = queries.shape[1], queries.shape[2]
    keys = keys_values.shape[1]
    half = width // 2
    heads = half // HD
    targets = NY * NZ * 8
    anywhere = pl.BlockSpec(memory_space=pl.ANY)
    vmem = pl.BlockSpec(memory_space=pltpu.VMEM)
    smem = pl.BlockSpec(memory_space=pltpu.SMEM)
    stats = (3, heads, targets)
    bf = lambda *shape: pltpu.VMEM(shape, BF)
    f32 = lambda *shape: pltpu.VMEM(shape, F32)
    dma = lambda *shape: pltpu.SemaphoreType.DMA(shape)
    return pl.pallas_call(
        kernel,
        out_shape=(
            jax.ShapeDtypeStruct(queries.shape, BF),
            jax.ShapeDtypeStruct(queries.shape, BF),
            jax.ShapeDtypeStruct(keys_values.shape, BF),
        ),
        in_specs=[anywhere, anywhere, smem, smem, anywhere],
        out_specs=(vmem, vmem, anywhere),
        scratch_shapes=[
            bf(2, rows, width),
            bf(2 * NX, rows, half),
            bf(2 * NX, rows, half),
            f32(8, half),
            bf(2, 8, half),
            bf(2, 8, half),
            bf(2, 8, half),
            bf(NY, NZ, 2, 8, half),
            bf(2, heads, targets, HD),
            bf(2, heads, 2 * keys, HD),
            f32(heads, 2 * keys, targets),
            f32(heads, 2 * keys, targets),
            f32(*stats),
            f32(3, *stats),
            f32(*stats),
            f32(3, *stats),
            f32(*stats),
            f32(*stats),
            bf(heads, 2 * keys, targets),
            bf(heads, 2 * keys, targets),
            f32(2, heads, NY, NZ * 8, HD),
            bf(2, heads, 2, NZ * 8, HD),
            bf(2, heads, NZ * 8, HD),
            bf(2, heads, NZ * 8, HD),
            bf(2, heads, 2, NZ * 8, HD),
            f32(2, NZ, 8, half),
            bf(2, 3, 2, 8, half),
            bf(2, 3, 2, 8, half),
            bf(2, 8, half),
            bf(2, 8, half),
            bf(2, 2, rows, half),
            bf(2 * NX, rows, half),
            bf(2 * NX, rows, half),
            bf(2, rows, width),
            bf(2, rows, width),
            bf(2, heads, 2 * keys, HD),
            dma(4 + 4 * heads),
            dma(2 * NX, 2), dma(2 * NX, 2),
            dma(2, heads), dma(2, heads),
            dma(2), dma(2),
            dma(NZ, 2), dma(NZ, 2),
            dma(3, NZ, 2), dma(3, NZ, 2),
            dma(7), dma(7),
            dma(2, heads, 3), dma(2, heads, 3),
            dma(2, 4), dma(2, 4),
            dma(2 * NX, 2), dma(2 * NX, 2),
            dma(2, heads), dma(2, heads),
        ],
        compiler_params=pltpu.CompilerParams(
            collective_id=0, has_side_effects=True, vmem_limit_bytes=56 * 1024 * 1024
        ),
    )(queries, keys_values, enc_len, order, d_out)


def solution(mesh):
    placed = (
        P("section", "seq", None),
        P("section", "seq", None),
        P("section"),
        P(),
        P("section", "seq", None),
    )
    return jax.shard_map(
        shards,
        mesh=mesh,
        in_specs=placed,
        out_specs=(P("section", "seq", None), P("section", "seq", None), P("section", "seq", None)),
        check_vma=False,
    )
```

time: 1210 us -> 93.2 us (0.08); the launches traced: 1190 us -> 92.8 us
  blocking collectives: 939 us -> 0 us
  waiting for transfers between devices: 124 us -> 0 us
  Pallas kernels: 0 us -> 85.7 us
  other arithmetic: 57.8 us -> 0 us
  starting transfers between devices: 19.4 us -> 0 us
  local copies, waits for them, and re-layouts: 24.1 us -> 5.79 us
  between operations: 15.6 us -> 1.29 us
  matrix products: 12.1 us -> 0 us
    unnamed x1 -> x0, blocking collectives: 462 us -> none
    all_gather x2 -> x0, blocking collectives: 234 us -> none  [combined_all(): everything = jax.tree.map(lambda part: lax.all_gather(part, axis), shard)]
    psum x1 -> x0, blocking collectives: 212 us -> none  [shards(): delta = lax.psum(jnp.sum(probabilities * dprobs, axis=-1), 'seq')]
    all_gather x2 -> x0, waiting for transfers between devices: 97.5 us -> none  [the longest x1 97.5 us: shards(): lax.all_gather(query_local, 'seq', axis=0, tiled=True)]
    pallas_call x0 -> x1, Pallas kernels: none -> 85.7 us  [shards(): pl.pallas_call(kernel, out_shape=(jax.ShapeDtypeStruct(queries.shape, BF)...]
    add x63 -> x0, other arithmetic: 46.1 us -> none  [combine_stats(): first[1] * jnp.exp(first[0] - top) + second[1] * jnp.exp(second[0] - top)]
    all_to_all x1 -> x0, blocking collectives: 32.1 us -> none  [shards(): lax.all_to_all(query_send, 'section', split_axis=0, concat_axis=0, tiled=...]
    all_to_all x3 -> x0, waiting for transfers between devices: 26.9 us -> none  [the longest x1 12.1 us: shards(): lax.all_to_all(queries_back, 'section', split_axis=0, concat_axis=0, tile...]
  transfers between devices with their start and end apart: 5 -> 0, of which waited for: 4 -> 0; matrix products, arithmetic and copies ran while one was open for 6% -> 0% of each run, Pallas kernels for 0% -> 0%
where the time goes in v1:
time: 93.2 us; the launch traced here: 92.8 us
  Pallas kernels  85.7 us (92%)
  local copies, waits for them, and re-layouts  5.79 us (6%)
  between operations  1.29 us (1%)
    pallas_call x1, Pallas kernels, shards(): pl.pallas_call(kernel, out_shape=(jax.ShapeDtypeStruct(queries.shape, BF)...  85.7 us
    unnamed x3, local copies, waits for them, and re-layouts  5.79 us

profile of v1, /device:TPU:1, one launch (start us, length us, event | category | flops | bytes accessed | tf_op | source)
XLA Modules:
  0.0 92.8 jit_solution(6718890624231788518)
XLA Ops:
  1.3 85.7 %shard_map.76 = (bf16[1,4,2048]{2,1,0:T(4,128)(2,1)}, bf16[1,4,2048]{2,1,0:T(4,128)(2,1)}, bf16[1,256,4096]{2,1,0:T(8,128)(2,1)}) custom-call(bf16[1,4,2048]{2,1,0:T(4,128)(2,1)} %q_ref.1, bf16[1,256,4096]{2,1,0:T(8,128)(2,1)} %kv_ref.1, s32[1]{0:T(128)S(6)} %copy.11.len_ref, s32[8]{0:T(128)} %ord_ref.1, bf16[1,4,2048]{2,1,0:T(4,128)(2,1)} %g_ref.1), custom_call_target="tpu_custom_call" | custom-call | tf_op jit(solution)/shard_map/pallas_call | solution.py:379
  87.0 1.3 %copy.12 = bf16[1,4,2048]{2,1,0:T(4,128)(2,1)} copy(bf16[1,4,2048]{2,1,0:T(4,128)(2,1)} %get-tuple-element.6) | data formatting | bytes 32768
  88.3 1.3 %copy.13 = bf16[1,4,2048]{2,1,0:T(4,128)(2,1)} copy(bf16[1,4,2048]{2,1,0:T(4,128)(2,1)} %get-tuple-element.7) | data formatting | bytes 32768
  89.7 3.1 %copy.14 = bf16[1,256,4096]{2,1,0:T(8,128)(2,1)} copy(bf16[1,256,4096]{2,1,0:T(8,128)(2,1)} %get-tuple-element.8) | data formatting | bytes 4194304

commit v2 on v0

v2 whole, which is shorter than its diff:
```python
import functools
import math

import jax
import jax.numpy as jnp
from jax import lax
from jax.experimental import pallas as pl
from jax.experimental.pallas import tpu as pltpu
from jax.sharding import PartitionSpec as P

MESH = pl.DeviceIdType.MESH
HD = 256
NX, NY, NZ = 4, 4, 8
OFFSETS = (0, 1, -1, 2)
BF = jnp.bfloat16
F32 = jnp.float32


def mod(a, n):
    return lax.rem(a, jnp.int32(n))


def merge(parts):
    top = functools.reduce(jnp.maximum, [p[0] for p in parts])
    scale = [jnp.exp(p[0] - top) for p in parts]
    total = sum(p[1] * s for p, s in zip(parts, scale))
    dots = sum(p[2] * s for p, s in zip(parts, scale))
    return top, total, dots


def kernel(
    q_ref, kv_ref, len_ref, ord_hbm, g_ref,
    att_ref, dq_ref, dkv_ref,
    qv, xb, rows32, sb, own, pb, gb, kvv, krel, ev, dv, st, szc, st2, szq,
    wv, dsv, of, zs, zq, zt, zc, rt, rb, psd, prb, dks, drel, ord_ref,
    load_sem, xs_sem, xr_sem, kvs_sem, kvr_sem, rs_sem, rr_sem, ps_sem, pr_sem, zs_sem, zr_sem,
    ss_sem, sr_sem, bs_sem, br_sem, ts_sem, tr_sem, ds_sem, dr_sem, es_sem, er_sem,
):
    sec = lax.axis_index("section")
    seq = lax.axis_index("seq")
    x, h = lax.div(sec, jnp.int32(2)), mod(sec, 2)
    y, zl, c = lax.div(seq, jnp.int32(16)), mod(lax.div(seq, jnp.int32(2)), NZ), mod(seq, 2)
    rows = q_ref.shape[1]
    width = q_ref.shape[2]
    keys = kv_ref.shape[1]
    nh = width // HD
    score_scale = 1.0 / math.sqrt(HD)
    quad, zin = lax.div(zl, jnp.int32(4)) * 4, mod(zl, 4)
    zx = mod(zl + 4, NZ)
    other = 1 - c
    me = y * 2 + c
    twin = x * 2 + (1 - h)

    def dev(xx, hh, yy, zz, cc):
        return (xx * 2 + hh, (yy * NZ + zz) * 2 + cc)

    def zto(d):
        return quad + mod(zin + d, 4)

    def zfrom(d):
        return quad + mod(zin + 4 - d, 4)

    def slot(r):
        base = zfrom(r % 4)
        return base if r < 4 else mod(base + 4, NZ)

    def ynb(d):
        return mod(y + d + NY, NY)

    def core_of(dc):
        return c if dc == 0 else other

    def cols(b, head):
        return pl.ds(pl.multiple_of(b * width + head * HD, HD), HD)

    def block(yy, cc):
        return pl.ds(pl.multiple_of((yy * 2 + cc) * keys, keys), keys)

    crowd = [(dx, dy, dc) for dx in range(NX) for dy in range(NY) for dc in range(2)]
    others = [t for t in crowd if t != (0, 0, 0)]
    partner = dev(x, 1 - h, y, zx, c)
    pending = []
    local = []

    def send(src, dst, ssem, rsem, target):
        copy = pltpu.make_async_remote_copy(
            src_ref=src, dst_ref=dst, send_sem=ssem, recv_sem=rsem, device_id=target, device_id_type=MESH
        )
        copy.start()
        pending.append(copy)

    def arrive(dst, ssem, rsem):
        pltpu.make_async_remote_copy(
            src_ref=dst, dst_ref=dst, send_sem=ssem, recv_sem=rsem, device_id=partner, device_id_type=MESH
        ).wait_recv()

    barrier = pltpu.get_barrier_semaphore()
    peers = [dev(mod(x + dx, NX), h, ynb(dy), zl, core_of(dc)) for dx, dy, dc in others]
    peers += [dev(x, h, y, zto(d), c) for d in (1, 2, 3)]
    peers += [dev(x, h, y, zx, c), partner]
    for peer in peers:
        pl.semaphore_signal(barrier, inc=1, device_id=peer, device_id_type=MESH)
    load_q = [
        pltpu.make_async_copy(ref.at[0], qv.at[a], load_sem.at[a]) for a, ref in enumerate((q_ref, g_ref))
    ]
    load_order = pltpu.make_async_copy(ord_hbm, ord_ref, load_sem.at[7])
    for copy in load_q + [load_order]:
        copy.start()
    load_kv = [
        pltpu.make_async_copy(kv_ref.at[0, :, cols(b, me)], kvv.at[b, block(y, c)], load_sem.at[2 + b])
        for b in range(2)
    ]
    for copy in load_kv:
        copy.start()
    for copy in load_q + [load_order]:
        copy.wait()
    pl.semaphore_wait(barrier, len(peers))

    for k, (dx, dy, dc) in enumerate(crowd):
        if k == 0:
            continue
        head = ynb(dy) * 2 + core_of(dc)
        send(
            qv.at[:, :, cols(0, head)], xb.at[dx, me], xs_sem.at[k], xr_sem.at[k],
            dev(mod(x + dx, NX), h, ynb(dy), zl, core_of(dc)),
        )
    own_copy = pltpu.make_async_copy(qv.at[:, :, cols(0, me)], xb.at[0, me], load_sem.at[4])
    own_copy.start()

    for dc in range(2):
        for b, d in ((0, 1), (1, -1)):
            send(
                kv_ref.at[0, :, cols(b, ynb(2) * 2 + core_of(dc))], krel.at[b, dc], rs_sem.at[b, dc], rr_sem.at[b, dc],
                dev(x, h, ynb(d), zl, core_of(dc)),
            )
    for b in range(2):
        for dyi, dc in ((1, 0), (2, 0), (1, 1), (2, 1), (0, 1)):
            yy = ynb(OFFSETS[dyi])
            send(
                kv_ref.at[0, :, cols(b, yy * 2 + core_of(dc))], kvv.at[b, block(y, c)],
                kvs_sem.at[b, dyi, dc], kvr_sem.at[b, dyi, dc], dev(x, h, yy, zl, core_of(dc)),
            )

    def inverse(section):
        found = jnp.int32(0)
        for k in range(2 * NX):
            found = jnp.where(ord_ref[k] == section, jnp.int32(k), found)
        return found

    src_mine, src_twin = inverse(sec), inverse(twin)

    def steps_to(section):
        return mod(x - lax.div(section, jnp.int32(2)) + NX, NX)

    own_copy.wait()
    for k, (dx, dy, dc) in enumerate(crowd):
        if k:
            arrive(xb.at[dx, ynb(-dy) * 2 + core_of(dc)], xs_sem.at[k], xr_sem.at[k])
    for dst, section in ((sb, src_twin), (own, src_mine)):
        steps = steps_to(section)
        for a in range(2):
            for k in range(nh):
                rows32[a, k * rows : (k + 1) * rows, :] = xb[steps, k, a].astype(F32)
            dst[a] = rows32[a].astype(BF)
        if dst is sb:
            for a in range(2):
                send(sb.at[a], pb.at[a], ps_sem.at[a], pr_sem.at[a], partner)
    mine_here = mod(src_mine, 2) == h

    def to_quad(r, a):
        k = r // 4 * 4
        for d in (1, 3, 2):
            send(
                gb.at[slot(r), a], gb.at[slot(r), a], zs_sem.at[d + k, a], zr_sem.at[d + k, a],
                dev(x, h, y, zto(d), c),
            )

    def z_arrive(r, a):
        arrive(gb.at[slot(r), a], zs_sem.at[r, a], zr_sem.at[r, a])

    for a in range(2):
        arrive(pb.at[a], ps_sem.at[a], pr_sem.at[a])
        gb[zl, a] = jnp.where(mine_here, own[a], pb[a])
        send(gb.at[zl, a], gb.at[zl, a], zs_sem.at[4, a], zr_sem.at[4, a], dev(x, h, y, zx, c))
    for a in range(2):
        to_quad(0, a)
    for dc in range(2):
        for b, d in ((0, 1), (1, -1)):
            arrive(krel.at[b, dc], rs_sem.at[b, dc], rr_sem.at[b, dc])
            send(
                krel.at[b, dc], kvv.at[b, block(ynb(-d), core_of(dc))], kvs_sem.at[b, 3, dc], kvr_sem.at[b, 3, dc],
                dev(x, h, ynb(d), zl, c),
            )
    for a in range(2):
        z_arrive(4, a)
        to_quad(4, a)
    for a in range(2):
        for r in (1, 2, 3, 5, 6, 7):
            z_arrive(r, a)

    targets = NZ * nh * rows
    span = 2 * keys
    key_at = lax.broadcasted_iota(jnp.int32, (span, targets), 0) + zl * span
    nt = (((1,), (1,)), ((), ()))
    nn = (((1,), (0,)), ((), ()))
    tn = (((0,), (0,)), ((), ()))
    query_all = gb[:, 0].reshape(targets, HD)
    grad_all = gb[:, 1].reshape(targets, HD)

    def part(b, j):
        return kvv[b, j * span : (j + 1) * span]

    def kv_arrive(b):
        load_kv[b].wait()
        for dyi, dc in ((0, 1), (1, 0), (1, 1), (2, 0), (2, 1), (3, 0), (3, 1)):
            arrive(kvv.at[b, block(ynb(-OFFSETS[dyi]), core_of(dc))], kvs_sem.at[b, dyi, dc], kvr_sem.at[b, dyi, dc])

    kv_arrive(0)
    top = jnp.full((1, targets), -1e30, F32)
    for j in range(NY):
        scores = lax.dot_general(part(0, j), query_all, nt, preferred_element_type=F32) * score_scale
        scores = jnp.where(key_at + j * NZ * span < len_ref[0], scores, -jnp.inf)
        ev[j] = scores
        top = jnp.maximum(top, jnp.max(scores, axis=0, keepdims=True))
    kv_arrive(1)
    total = jnp.zeros((1, targets), F32)
    dots = jnp.zeros((1, targets), F32)
    for j in range(NY):
        e = jnp.exp(ev[j] - top)
        dp = lax.dot_general(part(1, j), grad_all, nt, preferred_element_type=F32)
        ev[j] = e
        dv[j] = dp
        total = total + jnp.sum(e, axis=0, keepdims=True)
        dots = dots + jnp.sum(e * dp, axis=0, keepdims=True)

    stats = (top, total, dots)
    for i in range(3):
        st[i : i + 1, :] = stats[i]
    send(st, szc, ss_sem.at[0], sr_sem.at[0], dev(x, h, y, zx, c))
    arrive(szc, ss_sem.at[0], sr_sem.at[0])
    stats = merge([stats, [szc[i : i + 1, :] for i in range(3)]])
    for i in range(3):
        st2[i : i + 1, :] = stats[i]
    for d in (1, 3, 2):
        send(st2, szq.at[d - 1], ss_sem.at[d], sr_sem.at[d], dev(x, h, y, zto(d), c))
    for d in (1, 2, 3):
        arrive(szq.at[d - 1], ss_sem.at[d], sr_sem.at[d])
    whole_max, whole_sum, whole_dots = merge(
        [stats] + [[szq[d, i : i + 1, :] for i in range(3)] for d in range(3)]
    )
    inv_sum = 1.0 / whole_sum
    delta = whole_dots * inv_sum
    factor = jnp.exp(st[0:1, :] - whole_max) * inv_sum

    for a in range(2):
        acc = jnp.zeros((targets, HD), F32)
        for j in range(NY):
            p = ev[j] * factor
            if a == 0:
                left = p.astype(BF)
                wv[j] = left
            else:
                left = (p * (dv[j] - delta) * score_scale).astype(BF)
                dsv[j] = left
            acc = acc + lax.dot_general(left, part(1 - a, j), tn, preferred_element_type=F32)
        of[a] = acc.reshape(NZ, nh * rows, HD)
        for d in (1, 3, 2):
            zs[a, d - 1, 0] = of[a, zto(d)].astype(BF)
            zs[a, d - 1, 1] = of[a, mod(zto(d) + 4, NZ)].astype(BF)
            send(zs.at[a, d - 1], zq.at[a, d - 1], bs_sem.at[a, d], br_sem.at[a, d], dev(x, h, y, zto(d), c))

    def piece(b, dyi, dc):
        return dks.at[b, dyi, pl.ds(pl.multiple_of(core_of(dc) * keys, keys), keys)]

    def direct(b, dyi, dc):
        send(
            piece(b, dyi, dc), dkv_ref.at[0, :, cols(b, me)], ds_sem.at[b, dyi, dc], dr_sem.at[b, dyi, dc],
            dev(x, h, ynb(OFFSETS[dyi]), zl, core_of(dc)),
        )

    for dyi in (3, 1, 2, 0):
        j = ynb(OFFSETS[dyi])
        for b in (1, 0):
            right = grad_all if b else query_all
            grad = lax.dot_general((dsv, wv)[b][j], right, nn, preferred_element_type=F32)
            dks[b, dyi] = grad.astype(BF)
            d = 1 if b == 0 else -1
            for dc in range(2):
                if dyi == 3:
                    send(
                        piece(b, dyi, dc), drel.at[b, dc], es_sem.at[b, dc], er_sem.at[b, dc],
                        dev(x, h, ynb(d), zl, core_of(dc)),
                    )
                elif dyi == 0 and dc == 0:
                    copy = pltpu.make_async_copy(piece(b, 0, 0), dkv_ref.at[0, :, cols(b, me)], load_sem.at[5 + b])
                    copy.start()
                    local.append(copy)
                elif b == 1 or dyi == 0:
                    direct(b, dyi, dc)

    for a in range(2):
        for d in (1, 2, 3):
            arrive(zq.at[a, d - 1], bs_sem.at[a, d], br_sem.at[a, d])
        far = of[a, zx] + sum(zq[a, i, 1].astype(F32) for i in range(3))
        zt[a] = far.astype(BF)
        send(zt.at[a], zc.at[a], bs_sem.at[a, 0], br_sem.at[a, 0], dev(x, h, y, zx, c))
    for a in range(2):
        near = of[a, zl] + sum(zq[a, i, 0].astype(F32) for i in range(3))
        arrive(zc.at[a], bs_sem.at[a, 0], br_sem.at[a, 0])
        rows32[a] = near + zc[a].astype(F32)
        for k in range(nh):
            rt[k, a] = rows32[a, k * rows : (k + 1) * rows, :].astype(BF)
    for k, (dx, dy, dc) in enumerate(crowd):
        if k == 0:
            continue
        head = ynb(dy) * 2 + core_of(dc)
        send(
            rt.at[head], rb.at[dx, me], ts_sem.at[k], tr_sem.at[k],
            dev(mod(x + dx, NX), h, ynb(dy), zl, core_of(dc)),
        )
    rb[0, me] = rt[me]
    for dc in range(2):
        for b, d in ((0, 1), (1, -1)):
            arrive(drel.at[b, dc], es_sem.at[b, dc], er_sem.at[b, dc])
            send(
                drel.at[b, dc], dkv_ref.at[0, :, cols(b, ynb(-d) * 2 + core_of(dc))],
                ds_sem.at[b, 3, dc], dr_sem.at[b, 3, dc], dev(x, h, ynb(d), zl, c),
            )
    for dyi in (1, 2):
        for dc in range(2):
            direct(0, dyi, dc)

    for k, (dx, dy, dc) in enumerate(crowd):
        if k:
            arrive(rb.at[dx, ynb(-dy) * 2 + core_of(dc)], ts_sem.at[k], tr_sem.at[k])
    ran_mine, ran_twin = ord_ref[sec], ord_ref[twin]
    steps = steps_to(ran_twin)
    for a in range(2):
        for n in range(nh):
            psd[a, :, n * HD : (n + 1) * HD] = rb[steps, n, a]
    send(psd, prb, ts_sem.at[0], tr_sem.at[0], partner)
    ran_here = mod(ran_mine, 2) == h
    steps = steps_to(ran_mine)
    arrive(prb, ts_sem.at[0], tr_sem.at[0])
    for a, out in enumerate((att_ref, dq_ref)):
        for n in range(nh):
            part_cols = slice(n * HD, (n + 1) * HD)
            out[0, :, part_cols] = jnp.where(ran_here, rb[steps, n, a], prb[a, :, part_cols])
    for copy in local:
        copy.wait()
    for b in range(2):
        for dyi in range(NY):
            for dc in range(2):
                if dyi or dc:
                    head = ynb(-OFFSETS[dyi]) * 2 + core_of(dc)
                    arrive(dkv_ref.at[0, :, cols(b, head)], ds_sem.at[b, dyi, dc], dr_sem.at[b, dyi, dc])
    for copy in pending:
        copy.wait_send()


def writer(*refs):
    ins, outs, sem = refs[:3], refs[3:6], refs[6]
    copies = [pltpu.make_async_copy(i, o, sem.at[n]) for n, (i, o) in enumerate(zip(ins, outs))]
    for copy in copies:
        copy.start()
    for copy in copies:
        copy.wait()


def shards(queries, keys_values, enc_len, order, d_out):
    rows, width = queries.shape[1], queries.shape[2]
    keys = keys_values.shape[1]
    nh = width // HD
    group = nh * rows
    targets = NZ * group
    anywhere = pl.BlockSpec(memory_space=pl.ANY)
    smem = pl.BlockSpec(memory_space=pltpu.SMEM)
    in_hbm = pl.BlockSpec(memory_space=pltpu.HBM)
    vmem = pl.BlockSpec(memory_space=pltpu.VMEM)
    bf = lambda *shape: pltpu.VMEM(shape, BF)
    f32 = lambda *shape: pltpu.VMEM(shape, F32)
    dma = lambda *shape: pltpu.SemaphoreType.DMA(shape)
    shapes = (queries.shape, queries.shape, keys_values.shape)
    pinned = lambda t: pltpu.with_memory_space_constraint(t, pltpu.HBM)
    held = pl.pallas_call(
        kernel,
        out_shape=tuple(pltpu.VMEM(s, BF) for s in shapes),
        in_specs=[in_hbm, in_hbm, smem, in_hbm, in_hbm],
        out_specs=(vmem, vmem, vmem),
        scratch_shapes=[
            bf(2, rows, width),
            bf(NX, nh, 2, rows, HD),
            f32(2, group, HD),
            bf(2, group, HD),
            bf(2, group, HD),
            bf(2, group, HD),
            bf(NZ, 2, group, HD),
            bf(2, 8 * keys, HD),
            bf(2, 2, keys, HD),
            f32(NY, 2 * keys, targets),
            f32(NY, 2 * keys, targets),
            f32(4, targets),
            f32(4, targets),
            f32(4, targets),
            f32(3, 4, targets),
            bf(NY, 2 * keys, targets),
            bf(NY, 2 * keys, targets),
            f32(2, NZ, group, HD),
            bf(2, 3, 2, group, HD),
            bf(2, 3, 2, group, HD),
            bf(2, group, HD),
            bf(2, group, HD),
            bf(nh, 2, rows, HD),
            bf(NX, nh, 2, rows, HD),
            bf(2, rows, width),
            bf(2, rows, width),
            bf(2, NY, 2 * keys, HD),
            bf(2, 2, keys, HD),
            pltpu.SMEM(order.shape, jnp.int32),
            dma(8),
            dma(32), dma(32),
            dma(2, NY, 2), dma(2, NY, 2),
            dma(2, 2), dma(2, 2),
            dma(2), dma(2),
            dma(NZ, 2), dma(NZ, 2),
            dma(4), dma(4),
            dma(2, 4), dma(2, 4),
            dma(32), dma(32),
            dma(2, NY, 2), dma(2, NY, 2),
            dma(2, 2), dma(2, 2),
        ],
        compiler_params=pltpu.CompilerParams(
            collective_id=0, has_side_effects=True, vmem_limit_bytes=48 * 1024 * 1024
        ),
    )(*(pinned(t) if t is not enc_len else t for t in (queries, keys_values, enc_len, order, d_out)))
    return pl.pallas_call(
        writer,
        out_shape=tuple(jax.ShapeDtypeStruct(s, BF) for s in shapes),
        in_specs=[vmem] * 3,
        out_specs=(anywhere,) * 3,
        scratch_shapes=[dma(3)],
    )(*(pltpu.with_memory_space_constraint(t, pltpu.VMEM) for t in held))


def solution(mesh):
    placed = (
        P("section", "seq", None),
        P("section", "seq", None),
        P("section"),
        P(),
        P("section", "seq", None),
    )
    return jax.shard_map(
        shards,
        mesh=mesh,
        in_specs=placed,
        out_specs=(P("section", "seq", None), P("section", "seq", None), P("section", "seq", None)),
        check_vma=False,
    )
```

time: 1210 us -> 81.4 us (0.07); the launches traced: 1190 us -> 81.2 us
  blocking collectives: 939 us -> 0 us
  waiting for transfers between devices: 124 us -> 0 us
  Pallas kernels: 0 us -> 79.9 us
  other arithmetic: 57.8 us -> 0 us
  local copies, waits for them, and re-layouts: 24.1 us -> 0 us
  starting transfers between devices: 19.4 us -> 0 us
  between operations: 15.6 us -> 1.28 us
  matrix products: 12.1 us -> 0 us
    unnamed x1 -> x0, blocking collectives: 462 us -> none
    all_gather x2 -> x0, blocking collectives: 234 us -> none  [combined_all(): everything = jax.tree.map(lambda part: lax.all_gather(part, axis), shard)]
    psum x1 -> x0, blocking collectives: 212 us -> none  [shards(): delta = lax.psum(jnp.sum(probabilities * dprobs, axis=-1), 'seq')]
    all_gather x2 -> x0, waiting for transfers between devices: 97.5 us -> none  [the longest x1 97.5 us: shards(): lax.all_gather(query_local, 'seq', axis=0, tiled=True)]
    pallas_call x0 -> x2, Pallas kernels: none -> 79.9 us  [the longest x1 78.6 us: shards(): pl.pallas_call(kernel, out_shape=tuple((pltpu.VMEM(s, BF) for s in shapes...]
    add x63 -> x0, other arithmetic: 46.1 us -> none  [combine_stats(): first[1] * jnp.exp(first[0] - top) + second[1] * jnp.exp(second[0] - top)]
    all_to_all x1 -> x0, blocking collectives: 32.1 us -> none  [shards(): lax.all_to_all(query_send, 'section', split_axis=0, concat_axis=0, tiled=...]
    all_to_all x3 -> x0, waiting for transfers between devices: 26.9 us -> none  [the longest x1 12.1 us: shards(): lax.all_to_all(queries_back, 'section', split_axis=0, concat_axis=0, tile...]
  transfers between devices with their start and end apart: 5 -> 0, of which waited for: 4 -> 0; matrix products, arithmetic and copies ran while one was open for 6% -> 0% of each run, Pallas kernels for 0% -> 0%
where the time goes in v2:
time: 81.4 us; the launch traced here: 81.2 us
  Pallas kernels  79.9 us (98%)
  between operations  1.28 us (2%)
    pallas_call x1, Pallas kernels, shards(): pl.pallas_call(kernel, out_shape=tuple((pltpu.VMEM(s, BF) for s in shapes...  78.6 us

profile of v2, /device:TPU:1, one launch (start us, length us, event | category | flops | bytes accessed | tf_op | source)
XLA Modules:
  0.0 81.2 jit_solution(4351718736662579057)
XLA Ops:
  1.3 78.6 %shard_map.76 = (bf16[1,4,2048]{2,1,0:T(4,128)(2,1)S(1)}, bf16[1,4,2048]{2,1,0:T(4,128)(2,1)S(1)}, bf16[1,256,4096]{2,1,0:T(8,128)(2,1)S(1)}) custom-call(bf16[1,4,2048]{2,1,0:T(4,128)(2,1)} %q_ref.1, bf16[1,256,4096]{2,1,0:T(8,128)(2,1)} %kv_ref.1, s32[1]{0:T(128)S(6)} %copy.8.len_ref, s32[8]{0:T(128)} %ord_hbm.1, bf16[1,4,2048]{2,1,0:T(4,128)(2,1)} %g_ref.1), custom_call_target="tpu_custom_call" | custom-call | tf_op jit(solution)/shard_map/pallas_call | solution.py:385
  79.9 1.4 %shard_map.77 = (bf16[1,4,2048]{2,1,0:T(4,128)(2,1)}, bf16[1,4,2048]{2,1,0:T(4,128)(2,1)}, bf16[1,256,4096]{2,1,0:T(8,128)(2,1)}) custom-call(bf16[1,4,2048]{2,1,0:T(4,128)(2,1)S(1)} %get-tuple-element.6.refs_0_, bf16[1,4,2048]{2,1,0:T(4,128)(2,1)S(1)} %get-tuple-element.7.refs_1_, bf16[1,256,4096]{2,1,0:T(8,128)(2,1)S(1)} %get-tuple-element.8.refs_2_), custom_call_target="tpu_custom_call" | custom-call | tf_op jit(solution)/shard_map/pallas_call | solution.py:436

commit v3 on v2

v3 whole, which is shorter than its diff:
```python
import functools
import math

import jax
import jax.numpy as jnp
from jax import lax
from jax.experimental import pallas as pl
from jax.experimental.pallas import tpu as pltpu
from jax.sharding import PartitionSpec as P

MESH = pl.DeviceIdType.MESH
HD = 256
NX, NY, NZ = 4, 4, 8
OFFSETS = (0, 1, -1, 2)
BF = jnp.bfloat16
F32 = jnp.float32


def mod(a, n):
    return lax.rem(a, jnp.int32(n))


def merge(parts):
    top = functools.reduce(jnp.maximum, [p[0] for p in parts])
    scale = [jnp.exp(p[0] - top) for p in parts]
    total = sum(p[1] * s for p, s in zip(parts, scale))
    return top, total


def kernel(
    q_ref, kv_ref, len_ref, ord_hbm, g_ref,
    att_ref, dq_ref, dkv_ref,
    qv, xb, rows32, sb, own, pb, gb, kvv, krel, ev, dv, st, szc, st2, szq, dt, dtc, dt2, dtq,
    wv, dsv, of, zs, zq, zt, zc, rt, rb0, rb1, psd, prb, dks, drel, ord_ref,
    load_sem, xs_sem, xr_sem, kvs_sem, kvr_sem, rr_sem, ps_sem, pr_sem, zs_sem, zr_sem,
    ss_sem, sr_sem, bs_sem, br_sem, ts_sem, tr_sem, ds_sem, dr_sem, er_sem,
):
    sec = lax.axis_index("section")
    seq = lax.axis_index("seq")
    x, h = lax.div(sec, jnp.int32(2)), mod(sec, 2)
    y, zl, c = lax.div(seq, jnp.int32(16)), mod(lax.div(seq, jnp.int32(2)), NZ), mod(seq, 2)
    rows = q_ref.shape[1]
    width = q_ref.shape[2]
    keys = kv_ref.shape[1]
    nh = width // HD
    score_scale = 1.0 / math.sqrt(HD)
    quad, zin = lax.div(zl, jnp.int32(4)) * 4, mod(zl, 4)
    zx = mod(zl + 4, NZ)
    other = 1 - c
    rb = (rb0, rb1)
    me = y * 2 + c
    twin = x * 2 + (1 - h)

    def dev(xx, hh, yy, zz, cc):
        return (xx * 2 + hh, (yy * NZ + zz) * 2 + cc)

    def zto(d):
        return quad + mod(zin + d, 4)

    def zfrom(d):
        return quad + mod(zin + 4 - d, 4)

    def slot(r):
        base = zfrom(r % 4)
        return base if r < 4 else mod(base + 4, NZ)

    def ynb(d):
        return mod(y + d + NY, NY)

    def core_of(dc):
        return c if dc == 0 else other

    def cols(b, head):
        return pl.ds(pl.multiple_of(b * width + head * HD, HD), HD)

    def block(b, yy, cc):
        return pl.ds(pl.multiple_of((b * nh + yy * 2 + cc) * keys, keys), keys)

    def pair(b, yy):
        return pl.ds(pl.multiple_of((b * nh + yy * 2) * keys, 2 * keys), 2 * keys)

    crowd = [(dx, dy, dc) for dx in range(NX) for dy in range(NY) for dc in range(2)]
    others = [t for t in crowd if t != (0, 0, 0)]
    partner = dev(x, 1 - h, y, zx, c)
    local = []

    def send(src, dst, ssem, rsem, target):
        copy = pltpu.make_async_remote_copy(
            src_ref=src, dst_ref=dst, send_sem=ssem, recv_sem=rsem, device_id=target, device_id_type=MESH
        )
        copy.start()

    def arrive(dst, rsem):
        pltpu.make_async_remote_copy(
            src_ref=dst, dst_ref=dst, send_sem=tr_sem.at[0, 0], recv_sem=rsem, device_id=partner, device_id_type=MESH
        ).wait_recv()

    def sent(src, ssem):
        pltpu.make_async_remote_copy(
            src_ref=src, dst_ref=src, send_sem=ssem, recv_sem=tr_sem.at[0, 0], device_id=partner, device_id_type=MESH
        ).wait_send()

    barrier = pltpu.get_barrier_semaphore()
    peers = [dev(mod(x + dx, NX), h, ynb(dy), zl, core_of(dc)) for dx, dy, dc in others]
    peers += [dev(x, h, y, zto(d), c) for d in (1, 2, 3)]
    peers += [dev(x, h, y, zx, c), partner]
    for peer in peers:
        pl.semaphore_signal(barrier, inc=1, device_id=peer, device_id_type=MESH)
    load_q = [
        pltpu.make_async_copy(ref.at[0], qv.at[a], load_sem.at[a]) for a, ref in enumerate((q_ref, g_ref))
    ]
    load_order = pltpu.make_async_copy(ord_hbm, ord_ref, load_sem.at[7])
    for copy in load_q + [load_order]:
        copy.start()
    load_kv = [
        pltpu.make_async_copy(kv_ref.at[0, :, cols(b, me)], kvv.at[block(b, y, c)], load_sem.at[2 + b])
        for b in range(2)
    ]
    for copy in load_kv:
        copy.start()
    for copy in load_q + [load_order]:
        copy.wait()
    pl.semaphore_wait(barrier, len(peers))

    for dx, dy, dc in others:
        head = ynb(dy) * 2 + core_of(dc)
        send(
            qv.at[:, :, cols(0, head)], xb.at[dx * nh + me], xs_sem, xr_sem,
            dev(mod(x + dx, NX), h, ynb(dy), zl, core_of(dc)),
        )
    own_copy = pltpu.make_async_copy(qv.at[:, :, cols(0, me)], xb.at[me], load_sem.at[4])
    own_copy.start()

    ways = (1, -1)

    def kv_far(b):
        for dc in range(2):
            send(
                kv_ref.at[0, :, cols(b, ynb(2) * 2 + core_of(dc))], krel.at[b, dc], kvs_sem.at[0], rr_sem.at[b],
                dev(x, h, ynb(ways[dc]), zl, core_of(dc)),
            )

    kv_far(0)
    kv_far(1)

    def kv_direct(b):
        for dyi, dc in ((1, 0), (2, 0), (1, 1), (2, 1), (0, 1)):
            yy = ynb(OFFSETS[dyi])
            send(
                kv_ref.at[0, :, cols(b, yy * 2 + core_of(dc))], kvv.at[block(b, y, c)],
                kvs_sem.at[0], kvr_sem.at[b, dyi], dev(x, h, yy, zl, core_of(dc)),
            )

    def inverse(section):
        found = jnp.int32(0)
        for k in range(2 * NX):
            found = jnp.where(ord_ref[k] == section, jnp.int32(k), found)
        return found

    src_mine, src_twin = inverse(sec), inverse(twin)

    def steps_to(section):
        return mod(x - lax.div(section, jnp.int32(2)) + NX, NX) * nh

    own_copy.wait()
    arrive(xb.at[pl.ds(0, NX * nh - 1)], xr_sem)
    for dst, section in ((sb, src_twin), (own, src_mine)):
        steps = steps_to(section)
        for a in range(2):
            for k in range(nh):
                rows32[a, k * rows : (k + 1) * rows, :] = xb[steps + k, a].astype(F32)
            dst[a] = rows32[a].astype(BF)
            if dst is sb:
                send(sb.at[a], pb.at[a], ps_sem, pr_sem.at[a], partner)
        if dst is sb:
            kv_direct(0)
    mine_here = mod(src_mine, 2) == h

    chunks = [ynb(-d) for d in OFFSETS]

    def kv_arrive(b):
        load_kv[b].wait()
        arrive(kvv.at[block(b, y, other)], kvr_sem.at[b, 0])
        for dyi in (1, 2, 3):
            arrive(kvv.at[pair(b, chunks[dyi])], kvr_sem.at[b, dyi])

    def to_quad(r, a):
        for d in (1, 3, 2):
            send(gb.at[slot(r), a], gb.at[slot(r), a], zs_sem, zr_sem.at[2], dev(x, h, y, zto(d), c))

    for a in range(2):
        arrive(pb.at[a], pr_sem.at[a])
        gb[zl, a] = jnp.where(mine_here, own[a], pb[a])
        send(gb.at[zl, a], gb.at[zl, a], zs_sem, zr_sem.at[a], dev(x, h, y, zx, c))
    for a in range(2):
        to_quad(0, a)
    def kv_forward(b):
        arrive(krel.at[b], rr_sem.at[b])
        for dc, d in enumerate(ways):
            send(
                krel.at[b, dc], kvv.at[block(b, ynb(-d), core_of(dc))], kvs_sem.at[1], kvr_sem.at[b, 3],
                dev(x, h, ynb(d), zl, c),
            )

    kv_forward(0)
    kv_direct(1)
    for a in range(2):
        arrive(gb.at[zx, a], zr_sem.at[a])
        to_quad(4, a)
    kv_forward(1)
    kv_arrive(0)
    arrive(gb.at[pl.ds(0, NZ - 2)], zr_sem.at[2])

    targets = NZ * nh * rows
    span = 2 * keys
    key_at = lax.broadcasted_iota(jnp.int32, (span, targets), 0) + zl * span
    nt = (((1,), (1,)), ((), ()))
    nn = (((1,), (0,)), ((), ()))
    tn = (((0,), (0,)), ((), ()))
    query_all = gb[:, 0].reshape(targets, HD)
    grad_all = gb[:, 1].reshape(targets, HD)

    top = jnp.full((1, targets), -1e30, F32)
    for dyi, j in enumerate(chunks):
        scores = lax.dot_general(kvv[pair(0, j)], query_all, nt, preferred_element_type=F32) * score_scale
        scores = jnp.where(key_at + j * (NZ * span) < len_ref[0], scores, -jnp.inf)
        ev[dyi] = scores
        top = jnp.maximum(top, jnp.max(scores, axis=0, keepdims=True))
    total = jnp.zeros((1, targets), F32)
    for dyi in range(NY):
        e = jnp.exp(ev[dyi] - top)
        ev[dyi] = e
        total = total + jnp.sum(e, axis=0, keepdims=True)

    def put(ref, values):
        for i, value in enumerate(values):
            ref[i : i + 1, :] = value

    put(st, (top, total))
    send(st, szc, ss_sem.at[0], sr_sem.at[0], dev(x, h, y, zx, c))
    arrive(szc, sr_sem.at[0])
    stats = merge([(top, total), (szc[0:1, :], szc[1:2, :])])
    put(st2, stats)
    for d in (1, 3, 2):
        send(st2, szq.at[d - 1], ss_sem.at[0], sr_sem.at[1], dev(x, h, y, zto(d), c))
    kv_arrive(1)
    for dyi, j in enumerate(chunks):
        dv[dyi] = lax.dot_general(kvv[pair(1, j)], grad_all, nt, preferred_element_type=F32)
    arrive(szq.at[pl.ds(0, 3)], sr_sem.at[1])
    whole_max, whole_sum = merge([stats] + [(szq[d, 0:1, :], szq[d, 1:2, :]) for d in range(3)])
    factor = jnp.exp(top - whole_max) / whole_sum

    dots = jnp.zeros((1, targets), F32)
    for dyi in range(NY):
        p = ev[dyi] * factor
        ev[dyi] = p
        wv[dyi] = p.astype(BF)
        dots = dots + jnp.sum(p * dv[dyi], axis=0, keepdims=True)
    dt[...] = jnp.broadcast_to(dots, dt.shape)
    send(dt, dtc, ss_sem.at[1], sr_sem.at[2], dev(x, h, y, zx, c))

    def direct(b, dyi, dc):
        send(
            piece(b, dyi, dc), dkv_ref.at[0, :, cols(b, me)], ds_sem.at[0], dr_sem,
            dev(x, h, ynb(OFFSETS[dyi]), zl, core_of(dc)),
        )

    def piece(b, dyi, dc):
        return dks.at[b, dyi, pl.ds(pl.multiple_of(core_of(dc) * keys, keys), keys)]

    def grads(b):
        left, right = ((dsv, query_all), (wv, grad_all))[b]
        for dyi in (3, 1, 2, 0):
            held = {1: 2, 2: 1}.get(dyi, dyi)
            dks[b, dyi] = lax.dot_general(left[held], right, nn, preferred_element_type=F32).astype(BF)
            for dc in range(2):
                if dyi == 3:
                    send(
                        piece(b, dyi, dc), drel.at[b, dc], ds_sem.at[0], er_sem.at[b],
                        dev(x, h, ynb(ways[dc]), zl, core_of(dc)),
                    )
                elif dyi == 0 and dc == 0:
                    copy = pltpu.make_async_copy(piece(b, 0, 0), dkv_ref.at[0, :, cols(b, me)], load_sem.at[5 + b])
                    copy.start()
                    local.append(copy)
                elif b == 1 or dyi == 0 or dc == 0:
                    direct(b, dyi, dc)

    def forward(b):
        arrive(drel.at[b], er_sem.at[b])
        for dc, d in enumerate(ways):
            send(
                drel.at[b, dc], dkv_ref.at[0, :, cols(b, ynb(-d) * 2 + core_of(dc))],
                ds_sem.at[1], dr_sem, dev(x, h, ynb(d), zl, c),
            )

    def sums(a):
        acc = jnp.zeros((targets, HD), F32)
        for dyi in range(NY):
            j = chunks[dyi]
            acc = acc + lax.dot_general((wv, dsv)[a][dyi], kvv[pair(1 - a, j)], tn, preferred_element_type=F32)
        of[a] = acc.reshape(NZ, nh * rows, HD)
        for d in (1, 3, 2):
            zs[a, d - 1, 0] = of[a, zto(d)].astype(BF)
            zs[a, d - 1, 1] = of[a, mod(zto(d) + 4, NZ)].astype(BF)
            send(zs.at[a, d - 1], zq.at[a, d - 1], bs_sem.at[0], br_sem.at[0, a], dev(x, h, y, zto(d), c))

    def across(a):
        arrive(zq.at[a], br_sem.at[0, a])
        far = of[a, zx] + sum(zq[a, i, 1].astype(F32) for i in range(3))
        zt[a] = far.astype(BF)
        send(zt.at[a], zc.at[a], bs_sem.at[1], br_sem.at[1, a], dev(x, h, y, zx, c))

    def home(a):
        near = of[a, zl] + sum(zq[a, i, 0].astype(F32) for i in range(3))
        arrive(zc.at[a], br_sem.at[1, a])
        rows32[a] = near + zc[a].astype(F32)
        for k in range(nh):
            rt[a, k] = rows32[a, k * rows : (k + 1) * rows, :].astype(BF)
        for dx, dy, dc in others:
            head = ynb(dy) * 2 + core_of(dc)
            send(
                rt.at[a, head], rb[a].at[dx * nh + me], ts_sem.at[0], tr_sem.at[0, a],
                dev(mod(x + dx, NX), h, ynb(dy), zl, core_of(dc)),
            )
        rb[a][me] = rt[a, me]

    ran_mine, ran_twin = ord_ref[sec], ord_ref[twin]

    def over(a):
        arrive(rb[a].at[pl.ds(0, NX * nh - 1)], tr_sem.at[0, a])
        steps = steps_to(ran_twin)
        for n in range(nh):
            psd[a, :, n * HD : (n + 1) * HD] = rb[a][steps + n]
        send(psd.at[a], prb.at[a], ts_sem.at[1], tr_sem.at[1, a], partner)

    def keep(a, out):
        steps = steps_to(ran_mine)
        arrive(prb.at[a], tr_sem.at[1, a])
        for n in range(nh):
            part_cols = slice(n * HD, (n + 1) * HD)
            out[0, :, part_cols] = jnp.where(mod(ran_mine, 2) == h, rb[a][steps + n], prb[a, :, part_cols])

    grads(1)
    sums(0)
    arrive(dtc, sr_sem.at[2])
    dots = dots + dtc[0:1, :]
    dt2[...] = jnp.broadcast_to(dots, dt2.shape)
    for d in (1, 3, 2):
        send(dt2, dtq.at[d - 1], ss_sem.at[1], sr_sem.at[3], dev(x, h, y, zto(d), c))
    across(0)
    arrive(dtq.at[pl.ds(0, 3)], sr_sem.at[3])
    delta = dots + dtq[0, 0:1, :] + dtq[1, 0:1, :] + dtq[2, 0:1, :]
    for dyi in range(NY):
        dsv[dyi] = (ev[dyi] * (dv[dyi] - delta) * score_scale).astype(BF)
    sums(1)
    grads(0)
    forward(1)
    home(0)
    across(1)
    home(1)
    over(0)
    forward(0)
    for dyi in (1, 2):
        direct(0, dyi, 1)
    keep(0, att_ref)
    over(1)
    keep(1, dq_ref)
    sent(xb.at[pl.ds(0, NX * nh - 1)], xs_sem)
    sent(kvv.at[pl.ds(0, 14 * keys)], kvs_sem.at[0])
    sent(kvv.at[pl.ds(0, 4 * keys)], kvs_sem.at[1])
    sent(sb, ps_sem)
    sent(gb.at[pl.ds(0, NZ - 1)], zs_sem)
    sent(szq, ss_sem.at[0])
    sent(dtq, ss_sem.at[1])
    sent(zs, bs_sem.at[0])
    sent(zt, bs_sem.at[1])
    sent(xb.at[pl.ds(0, NX * nh - 1)], ts_sem.at[0])
    sent(psd, ts_sem.at[1])
    for copy in local:
        copy.wait()
    arrive(dkv_ref.at[0, :, pl.ds(0, (2 * nh - 1) * HD - HD)], dr_sem)
    sent(kvv.at[pl.ds(0, 14 * keys)], ds_sem.at[0])
    sent(kvv.at[pl.ds(0, 4 * keys)], ds_sem.at[1])


def writer(*refs):
    ins, outs, sem = refs[:3], refs[3:6], refs[6]
    copies = [pltpu.make_async_copy(i, o, sem.at[n]) for n, (i, o) in enumerate(zip(ins, outs))]
    for copy in copies:
        copy.start()
    for copy in copies:
        copy.wait()


def shards(queries, keys_values, enc_len, order, d_out):
    rows, width = queries.shape[1], queries.shape[2]
    keys = keys_values.shape[1]
    nh = width // HD
    group = nh * rows
    targets = NZ * group
    anywhere = pl.BlockSpec(memory_space=pl.ANY)
    smem = pl.BlockSpec(memory_space=pltpu.SMEM)
    in_hbm = pl.BlockSpec(memory_space=pltpu.HBM)
    vmem = pl.BlockSpec(memory_space=pltpu.VMEM)
    bf = lambda *shape: pltpu.VMEM(shape, BF)
    f32 = lambda *shape: pltpu.VMEM(shape, F32)
    dma = lambda *shape: pltpu.SemaphoreType.DMA(shape)
    one = pltpu.SemaphoreType.DMA
    shapes = (queries.shape, queries.shape, keys_values.shape)
    pinned = lambda t: pltpu.with_memory_space_constraint(t, pltpu.HBM)
    held = pl.pallas_call(
        kernel,
        out_shape=tuple(pltpu.VMEM(s, BF) for s in shapes),
        in_specs=[in_hbm, in_hbm, smem, in_hbm, in_hbm],
        out_specs=(vmem, vmem, vmem),
        scratch_shapes=[
            bf(2, rows, width),
            bf(NX * nh, 2, rows, HD),
            f32(2, group, HD),
            bf(2, group, HD),
            bf(2, group, HD),
            bf(2, group, HD),
            bf(NZ, 2, group, HD),
            bf(2 * nh * keys, HD),
            bf(2, 2, keys, HD),
            f32(NY, 2 * keys, targets),
            f32(NY, 2 * keys, targets),
            f32(2, targets),
            f32(2, targets),
            f32(2, targets),
            f32(4, 2, targets),
            f32(2, targets),
            f32(2, targets),
            f32(2, targets),
            f32(4, 2, targets),
            bf(NY, 2 * keys, targets),
            bf(NY, 2 * keys, targets),
            f32(2, NZ, group, HD),
            bf(2, 3, 2, group, HD),
            bf(2, 3, 2, group, HD),
            bf(2, group, HD),
            bf(2, group, HD),
            bf(2, nh, rows, HD),
            bf(NX * nh, rows, HD),
            bf(NX * nh, rows, HD),
            bf(2, rows, width),
            bf(2, rows, width),
            bf(2, NY, 2 * keys, HD),
            bf(2, 2, keys, HD),
            pltpu.SMEM(order.shape, jnp.int32),
            dma(8),
            one, one,
            dma(2), dma(2, NY), dma(2),
            one, dma(2),
            one, dma(3),
            dma(2), dma(4),
            dma(2), dma(2, 2),
            dma(2), dma(2, 2),
            dma(2), one, dma(2),
        ],
        compiler_params=pltpu.CompilerParams(
            collective_id=0, has_side_effects=True, vmem_limit_bytes=48 * 1024 * 1024
        ),
    )(*(pinned(t) if t is not enc_len else t for t in (queries, keys_values, enc_len, order, d_out)))
    return pl.pallas_call(
        writer,
        out_shape=tuple(jax.ShapeDtypeStruct(s, BF) for s in shapes),
        in_specs=[vmem] * 3,
        out_specs=(anywhere,) * 3,
        scratch_shapes=[dma(3)],
    )(*(pltpu.with_memory_space_constraint(t, pltpu.VMEM) for t in held))


def solution(mesh):
    placed = (
        P("section", "seq", None),
        P("section", "seq", None),
        P("section"),
        P(),
        P("section", "seq", None),
    )
    return jax.shard_map(
        shards,
        mesh=mesh,
        in_specs=placed,
        out_specs=(P("section", "seq", None), P("section", "seq", None), P("section", "seq", None)),
        check_vma=False,
    )
```

time: 81.4 us -> 74.9 us (0.920)
  Pallas kernels: 79.9 us -> 73.4 us
    pallas_call x1, Pallas kernels: 78.6 us -> 72.1 us  [shards(): pl.pallas_call(kernel, out_shape=tuple((pltpu.VMEM(s, BF) for s in shapes...]
where the time goes in v3:
time: 74.9 us; the launch traced here: 74.7 us
  Pallas kernels  73.4 us (98%)
  between operations  1.28 us (2%)
    pallas_call x1, Pallas kernels, shards(): pl.pallas_call(kernel, out_shape=tuple((pltpu.VMEM(s, BF) for s in shapes...  72.1 us

profile of v3, /device:TPU:1, one launch (start us, length us, event | category | flops | bytes accessed | tf_op | source)
XLA Modules:
  0.0 74.7 jit_solution(17707693290310171935)
XLA Ops:
  1.3 72.1 %shard_map.76 = (bf16[1,4,2048]{2,1,0:T(4,128)(2,1)S(1)}, bf16[1,4,2048]{2,1,0:T(4,128)(2,1)S(1)}, bf16[1,256,4096]{2,1,0:T(8,128)(2,1)S(1)}) custom-call(bf16[1,4,2048]{2,1,0:T(4,128)(2,1)} %q_ref.1, bf16[1,256,4096]{2,1,0:T(8,128)(2,1)} %kv_ref.1, s32[1]{0:T(128)S(6)} %copy.8.len_ref, s32[8]{0:T(128)} %ord_hbm.1, bf16[1,4,2048]{2,1,0:T(4,128)(2,1)} %g_ref.1), custom_call_target="tpu_custom_call" | custom-call | tf_op jit(solution)/shard_map/pallas_call | solution.py:412
  73.3 1.4 %shard_map.77 = (bf16[1,4,2048]{2,1,0:T(4,128)(2,1)}, bf16[1,4,2048]{2,1,0:T(4,128)(2,1)}, bf16[1,256,4096]{2,1,0:T(8,128)(2,1)}) custom-call(bf16[1,4,2048]{2,1,0:T(4,128)(2,1)S(1)} %get-tuple-element.6.refs_0_, bf16[1,4,2048]{2,1,0:T(4,128)(2,1)S(1)} %get-tuple-element.7.refs_1_, bf16[1,256,4096]{2,1,0:T(8,128)(2,1)S(1)} %get-tuple-element.8.refs_2_), custom_call_target="tpu_custom_call" | custom-call | tf_op jit(solution)/shard_map/pallas_call | solution.py:466

commit v4 on v3

--- a/solution.py
+++ b/solution.py
@@ -20,17 +20,10 @@
     return lax.rem(a, jnp.int32(n))
 
 
-def merge(parts):
-    top = functools.reduce(jnp.maximum, [p[0] for p in parts])
-    scale = [jnp.exp(p[0] - top) for p in parts]
-    total = sum(p[1] * s for p, s in zip(parts, scale))
-    return top, total
-
-
 def kernel(
     q_ref, kv_ref, len_ref, ord_hbm, g_ref,
     att_ref, dq_ref, dkv_ref,
-    qv, xb, rows32, sb, own, pb, gb, kvv, krel, ev, dv, st, szc, st2, szq, dt, dtc, dt2, dtq,
+    qv, xb, rows32, sb, own, pb, gb, kvv, krel, ev, dv, st, szs, dt, dts,
     wv, dsv, of, zs, zq, zt, zc, rt, rb0, rb1, psd, prb, dks, drel, ord_ref,
     load_sem, xs_sem, xr_sem, kvs_sem, kvr_sem, rr_sem, ps_sem, pr_sem, zs_sem, zr_sem,
     ss_sem, sr_sem, bs_sem, br_sem, ts_sem, tr_sem, ds_sem, dr_sem, er_sem,
@@ -59,6 +52,9 @@
 
     def zfrom(d):
         return quad + mod(zin + 4 - d, 4)
+
+    def zat(r):
+        return zto(r % 4) if r < 4 else mod(zto(r % 4) + 4, NZ)
 
     def slot(r):
         base = zfrom(r % 4)
@@ -232,32 +228,30 @@
         ev[dyi] = e
         total = total + jnp.sum(e, axis=0, keepdims=True)
 
-    def put(ref, values):
-        for i, value in enumerate(values):
-            ref[i : i + 1, :] = value
-
-    put(st, (top, total))
-    send(st, szc, ss_sem.at[0], sr_sem.at[0], dev(x, h, y, zx, c))
-    arrive(szc, sr_sem.at[0])
-    stats = merge([(top, total), (szc[0:1, :], szc[1:2, :])])
-    put(st2, stats)
-    for d in (1, 3, 2):
-        send(st2, szq.at[d - 1], ss_sem.at[0], sr_sem.at[1], dev(x, h, y, zto(d), c))
+    st[0:1, :] = top
+    st[1:2, :] = total
+    for r in (7, 5, 6, 4, 3, 2, 1):
+        send(st, szs.at[r - 1], ss_sem.at[0], sr_sem.at[0], dev(x, h, y, zat(r), c))
     kv_arrive(1)
+    dots = jnp.zeros((1, targets), F32)
     for dyi, j in enumerate(chunks):
-        dv[dyi] = lax.dot_general(kvv[pair(1, j)], grad_all, nt, preferred_element_type=F32)
-    arrive(szq.at[pl.ds(0, 3)], sr_sem.at[1])
-    whole_max, whole_sum = merge([stats] + [(szq[d, 0:1, :], szq[d, 1:2, :]) for d in range(3)])
-    factor = jnp.exp(top - whole_max) / whole_sum
-
-    dots = jnp.zeros((1, targets), F32)
+        dp = lax.dot_general(kvv[pair(1, j)], grad_all, nt, preferred_element_type=F32)
+        dv[dyi] = dp
+        dots = dots + jnp.sum(ev[dyi] * dp, axis=0, keepdims=True)
+    dt[...] = jnp.broadcast_to(dots, dt.shape)
+    for r in (7, 5, 6, 4, 3, 2, 1):
+        send(dt, dts.at[r - 1], ss_sem.at[1], sr_sem.at[1], dev(x, h, y, zat(r), c))
+    arrive(szs, sr_sem.at[0])
+    tops = [top] + [szs[i, 0:1, :] for i in range(NZ - 1)]
+    whole_max = functools.reduce(jnp.maximum, tops)
+    scales = [jnp.exp(t - whole_max) for t in tops]
+    whole_sum = total * scales[0] + sum(szs[i, 1:2, :] * scales[i + 1] for i in range(NZ - 1))
+    inv_sum = 1.0 / whole_sum
+    factor = scales[0] * inv_sum
     for dyi in range(NY):
         p = ev[dyi] * factor
         ev[dyi] = p
         wv[dyi] = p.astype(BF)
-        dots = dots + jnp.sum(p * dv[dyi], axis=0, keepdims=True)
-    dt[...] = jnp.broadcast_to(dots, dt.shape)
-    send(dt, dtc, ss_sem.at[1], sr_sem.at[2], dev(x, h, y, zx, c))
 
     def direct(b, dyi, dc):
         send(
@@ -343,36 +337,32 @@
 
     grads(1)
     sums(0)
-    arrive(dtc, sr_sem.at[2])
-    dots = dots + dtc[0:1, :]
-    dt2[...] = jnp.broadcast_to(dots, dt2.shape)
-    for d in (1, 3, 2):
-        send(dt2, dtq.at[d - 1], ss_sem.at[1], sr_sem.at[3], dev(x, h, y, zto(d), c))
-    across(0)
-    arrive(dtq.at[pl.ds(0, 3)], sr_sem.at[3])
-    delta = dots + dtq[0, 0:1, :] + dtq[1, 0:1, :] + dtq[2, 0:1, :]
+    arrive(dts, sr_sem.at[1])
+    delta = dots * scales[0] + sum(dts[i, 0:1, :] * scales[i + 1] for i in range(NZ - 1))
+    delta = delta * inv_sum
     for dyi in range(NY):
         dsv[dyi] = (ev[dyi] * (dv[dyi] - delta) * score_scale).astype(BF)
     sums(1)
+    across(0)
     grads(0)
     forward(1)
+    across(1)
     home(0)
-    across(1)
     home(1)
     over(0)
     forward(0)
     for dyi in (1, 2):
         direct(0, dyi, 1)
+    over(1)
     keep(0, att_ref)
-    over(1)
     keep(1, dq_ref)
     sent(xb.at[pl.ds(0, NX * nh - 1)], xs_sem)
     sent(kvv.at[pl.ds(0, 14 * keys)], kvs_sem.at[0])
     sent(kvv.at[pl.ds(0, 4 * keys)], kvs_sem.at[1])
     sent(sb, ps_sem)
     sent(gb.at[pl.ds(0, NZ - 1)], zs_sem)
-    sent(szq, ss_sem.at[0])
-    sent(dtq, ss_sem.at[1])
+    sent(szs, ss_sem.at[0])
+    sent(dts, ss_sem.at[1])
     sent(zs, bs_sem.at[0])
     sent(zt, bs_sem.at[1])
     sent(xb.at[pl.ds(0, NX * nh - 1)], ts_sem.at[0])
@@ -386,7 +376,10 @@
 
 def writer(*refs):
     ins, outs, sem = refs[:3], refs[3:6], refs[6]
-    copies = [pltpu.make_async_copy(i, o, sem.at[n]) for n, (i, o) in enumerate(zip(ins, outs))]
+    step = ins[2].shape[1] // 8
+    parts = [(ins[2].at[0, pl.ds(i * step, step)], outs[2].at[0, pl.ds(i * step, step)]) for i in range(8)]
+    parts += list(zip(ins[:2], outs[:2]))
+    copies = [pltpu.make_async_copy(i, o, sem.at[n]) for n, (i, o) in enumerate(parts)]
     for copy in copies:
         copy.start()
     for copy in copies:
@@ -427,13 +420,9 @@
             f32(NY, 2 * keys, targets),
             f32(NY, 2 * keys, targets),
             f32(2, targets),
+            f32(NZ - 1, 2, targets),
             f32(2, targets),
-            f32(2, targets),
-            f32(4, 2, targets),
-            f32(2, targets),
-            f32(2, targets),
-            f32(2, targets),
-            f32(4, 2, targets),
+            f32(NZ - 1, 2, targets),
             bf(NY, 2 * keys, targets),
             bf(NY, 2 * keys, targets),
             f32(2, NZ, group, HD),
@@ -454,7 +443,7 @@
             dma(2), dma(2, NY), dma(2),
             one, dma(2),
             one, dma(3),
-            dma(2), dma(4),
+            dma(2), dma(2),
             dma(2), dma(2, 2),
             dma(2), dma(2, 2),
             dma(2), one, dma(2),
@@ -468,7 +457,7 @@
         out_shape=tuple(jax.ShapeDtypeStruct(s, BF) for s in shapes),
         in_specs=[vmem] * 3,
         out_specs=(anywhere,) * 3,
-        scratch_shapes=[dma(3)],
+        scratch_shapes=[dma(10)],
     )(*(pltpu.with_memory_space_constraint(t, pltpu.VMEM) for t in held))
 
 

time: 74.9 us -> 72.7 us (0.971)
  Pallas kernels: 73.4 us -> 71.2 us
    pallas_call x1, Pallas kernels: 72.1 us -> 69.8 us  [shards(): pl.pallas_call(kernel, out_shape=tuple((pltpu.VMEM(s, BF) for s in shapes...]
where the time goes in v4:
time: 72.7 us; the launch traced here: 72.5 us
  Pallas kernels  71.2 us (98%)
  between operations  1.28 us (2%)
    pallas_call x1, Pallas kernels, shards(): pl.pallas_call(kernel, out_shape=tuple((pltpu.VMEM(s, BF) for s in shapes...  69.8 us

profile of v4, /device:TPU:1, one launch (start us, length us, event | category | flops | bytes accessed | tf_op | source)
XLA Modules:
  0.0 72.5 jit_solution(12158371010174976107)
XLA Ops:
  1.3 69.8 %shard_map.76 = (bf16[1,4,2048]{2,1,0:T(4,128)(2,1)S(1)}, bf16[1,4,2048]{2,1,0:T(4,128)(2,1)S(1)}, bf16[1,256,4096]{2,1,0:T(8,128)(2,1)S(1)}) custom-call(bf16[1,4,2048]{2,1,0:T(4,128)(2,1)} %q_ref.1, bf16[1,256,4096]{2,1,0:T(8,128)(2,1)} %kv_ref.1, s32[1]{0:T(128)S(6)} %copy.8.len_ref, s32[8]{0:T(128)} %ord_hbm.1, bf16[1,4,2048]{2,1,0:T(4,128)(2,1)} %g_ref.1), custom_call_target="tpu_custom_call" | custom-call | tf_op jit(solution)/shard_map/pallas_call | solution.py:405
  71.1 1.4 %shard_map.77 = (bf16[1,4,2048]{2,1,0:T(4,128)(2,1)}, bf16[1,4,2048]{2,1,0:T(4,128)(2,1)}, bf16[1,256,4096]{2,1,0:T(8,128)(2,1)}) custom-call(bf16[1,4,2048]{2,1,0:T(4,128)(2,1)S(1)} %get-tuple-element.6.refs_0_, bf16[1,4,2048]{2,1,0:T(4,128)(2,1)S(1)} %get-tuple-element.7.refs_1_, bf16[1,256,4096]{2,1,0:T(8,128)(2,1)S(1)} %get-tuple-element.8.refs_2_), custom_call_target="tpu_custom_call" | custom-call | tf_op jit(solution)/shard_map/pallas_call | solution.py:455

commit v5 on v4

--- a/solution.py
+++ b/solution.py
@@ -277,7 +277,7 @@
                     copy = pltpu.make_async_copy(piece(b, 0, 0), dkv_ref.at[0, :, cols(b, me)], load_sem.at[5 + b])
                     copy.start()
                     local.append(copy)
-                elif b == 1 or dyi == 0 or dc == 0:
+                elif b == 1 or dyi == 0:
                     direct(b, dyi, dc)
 
     def forward(b):
@@ -349,10 +349,11 @@
     across(1)
     home(0)
     home(1)
+    forward(0)
+    for dc in range(2):
+        for dyi in (1, 2):
+            direct(0, dyi, dc)
     over(0)
-    forward(0)
-    for dyi in (1, 2):
-        direct(0, dyi, 1)
     over(1)
     keep(0, att_ref)
     keep(1, dq_ref)

time: 72.7 us -> 70.8 us (0.974)
  Pallas kernels: 71.2 us -> 69.3 us
    pallas_call x1, Pallas kernels: 69.8 us -> 67.9 us  [shards(): pl.pallas_call(kernel, out_shape=tuple((pltpu.VMEM(s, BF) for s in shapes...]
where the time goes in v5:
time: 70.8 us; the launch traced here: 70.6 us
  Pallas kernels  69.3 us (98%)
  between operations  1.28 us (2%)
    pallas_call x1, Pallas kernels, shards(): pl.pallas_call(kernel, out_shape=tuple((pltpu.VMEM(s, BF) for s in shapes...  67.9 us

profile of v5, /device:TPU:1, one launch (start us, length us, event | category | flops | bytes accessed | tf_op | source)
XLA Modules:
  0.0 70.6 jit_solution(7030812815766624117)
XLA Ops:
  1.3 67.9 %shard_map.76 = (bf16[1,4,2048]{2,1,0:T(4,128)(2,1)S(1)}, bf16[1,4,2048]{2,1,0:T(4,128)(2,1)S(1)}, bf16[1,256,4096]{2,1,0:T(8,128)(2,1)S(1)}) custom-call(bf16[1,4,2048]{2,1,0:T(4,128)(2,1)} %q_ref.1, bf16[1,256,4096]{2,1,0:T(8,128)(2,1)} %kv_ref.1, s32[1]{0:T(128)S(6)} %copy.8.len_ref, s32[8]{0:T(128)} %ord_hbm.1, bf16[1,4,2048]{2,1,0:T(4,128)(2,1)} %g_ref.1), custom_call_target="tpu_custom_call" | custom-call | tf_op jit(solution)/shard_map/pallas_call | solution.py:406
  69.2 1.4 %shard_map.77 = (bf16[1,4,2048]{2,1,0:T(4,128)(2,1)}, bf16[1,4,2048]{2,1,0:T(4,128)(2,1)}, bf16[1,256,4096]{2,1,0:T(8,128)(2,1)}) custom-call(bf16[1,4,2048]{2,1,0:T(4,128)(2,1)S(1)} %get-tuple-element.6.refs_0_, bf16[1,4,2048]{2,1,0:T(4,128)(2,1)S(1)} %get-tuple-element.7.refs_1_, bf16[1,256,4096]{2,1,0:T(8,128)(2,1)S(1)} %get-tuple-element.8.refs_2_), custom_call_target="tpu_custom_call" | custom-call | tf_op jit(solution)/shard_map/pallas_call | solution.py:456

commit v6 on v5

--- a/solution.py
+++ b/solution.py
@@ -182,7 +182,7 @@
 
     def to_quad(r, a):
         for d in (1, 3, 2):
-            send(gb.at[slot(r), a], gb.at[slot(r), a], zs_sem, zr_sem.at[2], dev(x, h, y, zto(d), c))
+            send(gb.at[slot(r), a], gb.at[slot(r), a], zs_sem, zr_sem.at[2 + a], dev(x, h, y, zto(d), c))
 
     for a in range(2):
         arrive(pb.at[a], pr_sem.at[a])
@@ -205,7 +205,7 @@
         to_quad(4, a)
     kv_forward(1)
     kv_arrive(0)
-    arrive(gb.at[pl.ds(0, NZ - 2)], zr_sem.at[2])
+    arrive(gb.at[pl.ds(0, NZ // 2 - 1)], zr_sem.at[2])
 
     targets = NZ * nh * rows
     span = 2 * keys
@@ -214,7 +214,6 @@
     nn = (((1,), (0,)), ((), ()))
     tn = (((0,), (0,)), ((), ()))
     query_all = gb[:, 0].reshape(targets, HD)
-    grad_all = gb[:, 1].reshape(targets, HD)
 
     top = jnp.full((1, targets), -1e30, F32)
     for dyi, j in enumerate(chunks):
@@ -232,22 +231,14 @@
     st[1:2, :] = total
     for r in (7, 5, 6, 4, 3, 2, 1):
         send(st, szs.at[r - 1], ss_sem.at[0], sr_sem.at[0], dev(x, h, y, zat(r), c))
-    kv_arrive(1)
-    dots = jnp.zeros((1, targets), F32)
-    for dyi, j in enumerate(chunks):
-        dp = lax.dot_general(kvv[pair(1, j)], grad_all, nt, preferred_element_type=F32)
-        dv[dyi] = dp
-        dots = dots + jnp.sum(ev[dyi] * dp, axis=0, keepdims=True)
-    dt[...] = jnp.broadcast_to(dots, dt.shape)
-    for r in (7, 5, 6, 4, 3, 2, 1):
-        send(dt, dts.at[r - 1], ss_sem.at[1], sr_sem.at[1], dev(x, h, y, zat(r), c))
+    arrive(gb.at[pl.ds(0, NZ // 2 - 1)], zr_sem.at[3])
+    grad_all = gb[:, 1].reshape(targets, HD)
     arrive(szs, sr_sem.at[0])
     tops = [top] + [szs[i, 0:1, :] for i in range(NZ - 1)]
     whole_max = functools.reduce(jnp.maximum, tops)
     scales = [jnp.exp(t - whole_max) for t in tops]
     whole_sum = total * scales[0] + sum(szs[i, 1:2, :] * scales[i + 1] for i in range(NZ - 1))
-    inv_sum = 1.0 / whole_sum
-    factor = scales[0] * inv_sum
+    factor = scales[0] / whole_sum
     for dyi in range(NY):
         p = ev[dyi] * factor
         ev[dyi] = p
@@ -262,9 +253,9 @@
     def piece(b, dyi, dc):
         return dks.at[b, dyi, pl.ds(pl.multiple_of(core_of(dc) * keys, keys), keys)]
 
-    def grads(b):
+    def grads(b, steps):
         left, right = ((dsv, query_all), (wv, grad_all))[b]
-        for dyi in (3, 1, 2, 0):
+        for dyi in steps:
             held = {1: 2, 2: 1}.get(dyi, dyi)
             dks[b, dyi] = lax.dot_general(left[held], right, nn, preferred_element_type=F32).astype(BF)
             for dc in range(2):
@@ -335,16 +326,25 @@
             part_cols = slice(n * HD, (n + 1) * HD)
             out[0, :, part_cols] = jnp.where(mod(ran_mine, 2) == h, rb[a][steps + n], prb[a, :, part_cols])
 
-    grads(1)
+    grads(1, (3, 1))
+    kv_arrive(1)
+    dots = jnp.zeros((1, targets), F32)
+    for dyi, j in enumerate(chunks):
+        dp = lax.dot_general(kvv[pair(1, j)], grad_all, nt, preferred_element_type=F32)
+        dv[dyi] = dp
+        dots = dots + jnp.sum(ev[dyi] * dp, axis=0, keepdims=True)
+    dt[...] = jnp.broadcast_to(dots, dt.shape)
+    for r in (7, 5, 6, 4, 3, 2, 1):
+        send(dt, dts.at[r - 1], ss_sem.at[1], sr_sem.at[1], dev(x, h, y, zat(r), c))
+    grads(1, (2, 0))
     sums(0)
     arrive(dts, sr_sem.at[1])
-    delta = dots * scales[0] + sum(dts[i, 0:1, :] * scales[i + 1] for i in range(NZ - 1))
-    delta = delta * inv_sum
+    delta = dots + sum(dts[i, 0:1, :] for i in range(NZ - 1))
     for dyi in range(NY):
         dsv[dyi] = (ev[dyi] * (dv[dyi] - delta) * score_scale).astype(BF)
     sums(1)
     across(0)
-    grads(0)
+    grads(0, (3, 1, 2, 0))
     forward(1)
     across(1)
     home(0)
@@ -443,7 +443,7 @@
             one, one,
             dma(2), dma(2, NY), dma(2),
             one, dma(2),
-            one, dma(3),
+            one, dma(4),
             dma(2), dma(2),
             dma(2), dma(2, 2),
             dma(2), dma(2, 2),

time: 70.8 us -> 70.2 us (level)
  no operation moved by 1% of the time
where the time goes in v6:
time: 70.2 us; the launch traced here: 70 us
  Pallas kernels  68.7 us (98%)
  between operations  1.28 us (2%)
    pallas_call x1, Pallas kernels, shards(): pl.pallas_call(kernel, out_shape=tuple((pltpu.VMEM(s, BF) for s in shapes...  67.4 us

profile of v6, /device:TPU:1, one launch (start us, length us, event | category | flops | bytes accessed | tf_op | source)
XLA Modules:
  0.0 70.0 jit_solution(5352205941162836008)
XLA Ops:
  1.3 67.4 %shard_map.76 = (bf16[1,4,2048]{2,1,0:T(4,128)(2,1)S(1)}, bf16[1,4,2048]{2,1,0:T(4,128)(2,1)S(1)}, bf16[1,256,4096]{2,1,0:T(8,128)(2,1)S(1)}) custom-call(bf16[1,4,2048]{2,1,0:T(4,128)(2,1)} %q_ref.1, bf16[1,256,4096]{2,1,0:T(8,128)(2,1)} %kv_ref.1, s32[1]{0:T(128)S(6)} %copy.8.len_ref, s32[8]{0:T(128)} %ord_hbm.1, bf16[1,4,2048]{2,1,0:T(4,128)(2,1)} %g_ref.1), custom_call_target="tpu_custom_call" | custom-call | tf_op jit(solution)/shard_map/pallas_call | solution.py:406
  68.6 1.4 %shard_map.77 = (bf16[1,4,2048]{2,1,0:T(4,128)(2,1)}, bf16[1,4,2048]{2,1,0:T(4,128)(2,1)}, bf16[1,256,4096]{2,1,0:T(8,128)(2,1)}) custom-call(bf16[1,4,2048]{2,1,0:T(4,128)(2,1)S(1)} %get-tuple-element.6.refs_0_, bf16[1,4,2048]{2,1,0:T(4,128)(2,1)S(1)} %get-tuple-element.7.refs_1_, bf16[1,256,4096]{2,1,0:T(8,128)(2,1)S(1)} %get-tuple-element.8.refs_2_), custom_call_target="tpu_custom_call" | custom-call | tf_op jit(solution)/shard_map/pallas_call | solution.py:456
